TPU v7x, 128 devices: a whole 4x4x4 slice. The times are simulated.
128 devices in a mesh: gx: 16 (over x, y_hi, core), gy: 8 (over y_lo, z).
Axes of the slice: x: 4, y: 4 (y_hi: 2, y_lo: 2; y = y_hi * 2 + y_lo), z: 4, core: 2. Of those that a mesh axis runs over, the one named last changes fastest.
Arguments:
- features: bfloat16 [16, 8, 2048, 256], P('gx', 'gy'), may hold values from -6 to 6
- neighbours: int32 [16, 8, 27, 2048], P('gx', 'gy'), may hold values from 0 to 2048, as said below
- counts: int32 [16, 8], P('gx', 'gy'), may hold values from 1024 to 2048, as said below
- block_dest: int32 [16, 8, 128], P('gx', 'gy'), may hold values from 0 to 16383, as said below
- conv_weight: bfloat16 [27, 256, 256], replicated, may hold values from -0.078125 to 0.078125
- cpe_weight: bfloat16 [256, 256], replicated, may hold values from -0.375 to 0.375
- cpe_gain: float32 [256], replicated, may hold values from 0.25 to 1.75
- norm1_gain: float32 [256], replicated, may hold values from 0.25 to 1.75
- qkv_weight: bfloat16 [256, 768], replicated
- proj_weight: bfloat16 [256, 256], replicated, may hold values from -0.375 to 0.375
- norm2_gain: float32 [256], replicated, may hold values from 0.25 to 1.75
- fc1_weight: bfloat16 [256, 1024], replicated, may hold values from -0.375 to 0.375
- fc2_weight: bfloat16 [1024, 256], replicated, may hold values from -0.1875 to 0.1875
Outputs:
- block_out: bfloat16 [16, 8, 2048, 256], P('gx', 'gy')
Inputs may be any that keep to these rules, and one draw needn't show every extreme that they name: `neighbours`: tap 13 of every row is the row itself; the value 2048 marks a missing neighbour; other values are rows of the same device. `counts`: every device has at least 1024 live rows; some device has exactly 2048 and some exactly 1024; the offset of every device but the first is not a multiple of 1024. `block_dest`: every value appears exactly once; the blocks of one device go to different devices.
All inputs are finite; a program needn't handle non-finite values.
Results may differ from a plain program's by a relative error of at most 0.0095.
The roundings to bfloat16 on the way count: a program that leaves them out, or rounds other values in their place, can miss the bound.
Values may be sent and summed in bfloat16 or wider, within the bound.
A program may use at most 448 MiB of HBM per device.

v0:
```python
import jax
import jax.numpy as jnp
from jax import lax
from jax.sharding import PartitionSpec as P

HEADS = 16
PATCH = 1024


def entering(value, axis, join, neutral):
    count, mine = (lax.axis_size(axis), lax.axis_index(axis))
    pieces = lax.all_gather(value, axis)
    so_far = jnp.full_like(value, 0) + jnp.asarray(neutral, value.dtype)

    def hop(position, so_far):
        longer = join(so_far, pieces[position])
        return jnp.where(position < mine, longer, so_far)

    return lax.fori_loop(0, count - 1, hop, so_far)


def passed_along(shard, axis, by):
    count = lax.axis_size(axis)
    pairs = [(i, i + by) for i in range(count) if 0 <= i + by < count]
    return lax.ppermute(shard, axis, pairs)


def layer_norm(values, scale_gain):
    centre = values - jnp.mean(values, axis=-1, keepdims=True)
    spread = jnp.mean(centre * centre, axis=-1, keepdims=True)
    return centre * lax.rsqrt(spread + 1e-05) * scale_gain


def attend_patch(queries, key_rows, value_rows, key_live):
    length = queries.shape[0]
    feat_width = queries.shape[1]
    head_dim = feat_width // HEADS
    group_width = min(128, feat_width)
    group_heads = group_width // head_dim
    pieces = []
    for group_index in range(feat_width // group_width):
        lo_col = group_index * group_width
        hi_col = lo_col + group_width
        q_part = queries[:, lo_col:hi_col].reshape(length, group_heads, head_dim)
        k_part = key_rows[:, lo_col:hi_col].reshape(length, group_heads, head_dim)
        v_part = value_rows[:, lo_col:hi_col].reshape(length, group_heads, head_dim)
        scores = jnp.einsum(
            "qhd,khd->hqk", q_part, k_part, preferred_element_type=jnp.float32
        ) * head_dim ** (-0.5)
        scores = jnp.where(key_live[None, None, :], scores, jnp.float32(-1e30))
        row_max = jnp.max(scores, axis=-1, keepdims=True)
        exp_scores = jnp.exp(scores - row_max)
        weights = (exp_scores / jnp.sum(exp_scores, axis=-1, keepdims=True)).astype(jnp.bfloat16)
        group_out = jnp.einsum("hqk,khd->qhd", weights, v_part, preferred_element_type=jnp.float32)
        pieces.append(group_out.astype(jnp.bfloat16).reshape(length, group_width))
    return jnp.concatenate(pieces, axis=1)


def add_counts(earlier, later):
    return earlier + later


def per_device(
    features,
    neighbours,
    counts,
    block_dest,
    conv_weight,
    cpe_weight,
    cpe_gain,
    norm1_gain,
    qkv_weight,
    proj_weight,
    norm2_gain,
    fc1_weight,
    fc2_weight,
):
    row_count = features.shape[2]
    feat_width = features.shape[3]
    tap_count = neighbours.shape[2]
    local_rows = features.reshape(row_count, feat_width)
    tap_rows = neighbours.reshape(tap_count * row_count)
    padded = jnp.concatenate([local_rows, jnp.zeros((1, feat_width), jnp.bfloat16)], axis=0)
    picked = jnp.take(padded, tap_rows, axis=0).reshape(tap_count, row_count, feat_width)
    summed = lax.dot_general(
        picked, conv_weight, (((0, 2), (0, 1)), ((), ())), preferred_element_type=jnp.float32
    )
    conv_out = summed.astype(jnp.bfloat16)
    linear = jnp.dot(conv_out, cpe_weight, preferred_element_type=jnp.float32)
    encoded = (local_rows.astype(jnp.float32) + layer_norm(linear, cpe_gain)).astype(jnp.bfloat16)
    block_count = block_dest.shape[2]
    block_span = row_count // block_count * feat_width
    size_gx = lax.axis_size("gx")
    size_gy = lax.axis_size("gy")
    devices = size_gx * size_gy
    block_target = block_dest.reshape(block_count)
    target = block_target // block_count
    slot_index = block_target % block_count
    outgoing = (
        jnp.zeros((devices, block_span), jnp.bfloat16)
        .at[target]
        .set(encoded.reshape(block_count, block_span))
    )
    labels = jnp.full((devices,), block_count, jnp.int32).at[target].set(slot_index)
    arrived, slot_tags = (
        lax.all_to_all(outgoing, ("gx", "gy"), split_axis=0, concat_axis=0, tiled=True),
        lax.all_to_all(labels, ("gx", "gy"), split_axis=0, concat_axis=0, tiled=True),
    )
    reordered = (
        jnp.zeros((block_count, block_span), jnp.bfloat16)
        .at[slot_tags]
        .set(arrived, mode="drop")
        .reshape(row_count, feat_width)
    )
    own_count = counts.reshape(1)
    live_count = own_count[0]
    before_sum = entering(own_count, ("gx", "gy"), add_counts, jnp.zeros((1,), jnp.int32))
    offset = before_sum[0].astype(jnp.int32)
    grand_total = lax.psum(own_count, ("gx", "gy"))[0]
    normed = layer_norm(reordered.astype(jnp.float32), norm1_gain).astype(jnp.bfloat16)
    projected = jnp.dot(normed, qkv_weight, preferred_element_type=jnp.float32).astype(jnp.bfloat16)
    queries = projected[:, :feat_width]
    key_pairs = projected[:, feat_width:]
    tail_pairs = lax.dynamic_slice_in_dim(key_pairs, live_count - PATCH, PATCH, 0)
    before_pairs = passed_along(tail_pairs, ("gx", "gy"), 1)
    after_pairs = passed_along(key_pairs[:PATCH], ("gx", "gy"), -1)
    patch_slots = -(-row_count // PATCH) + 1
    extent = (patch_slots + 1) * PATCH
    filler = extent - PATCH - row_count
    ext_pairs = jnp.concatenate(
        [before_pairs, key_pairs, jnp.zeros((filler, 2 * feat_width), jnp.bfloat16)], axis=0
    )
    ext_pairs = lax.dynamic_update_slice_in_dim(ext_pairs, after_pairs, PATCH + live_count, 0)
    ext_queries = jnp.concatenate(
        [
            jnp.zeros((PATCH, feat_width), jnp.bfloat16),
            queries,
            jnp.zeros((filler, feat_width), jnp.bfloat16),
        ],
        axis=0,
    )
    spot_index = jnp.arange(extent, dtype=jnp.int32)
    global_spot = offset - PATCH + spot_index
    key_live = (
        (global_spot >= 0) & (global_spot < grand_total) & (spot_index < 2 * PATCH + live_count)
    )
    first_start = PATCH - offset % PATCH
    results = []
    for patch_index in range(patch_slots):
        begin_row = first_start + patch_index * PATCH
        q_patch = lax.dynamic_slice_in_dim(ext_queries, begin_row, PATCH, 0)
        kv_patch = lax.dynamic_slice_in_dim(ext_pairs, begin_row, PATCH, 0)
        live_patch = lax.dynamic_slice_in_dim(key_live, begin_row, PATCH, 0)
        results.append(
            attend_patch(q_patch, kv_patch[:, :feat_width], kv_patch[:, feat_width:], live_patch)
        )
    joined = jnp.concatenate(results, axis=0)
    attended = lax.dynamic_slice_in_dim(joined, PATCH - first_start, row_count, 0)
    attended = jnp.where(
        (jnp.arange(row_count) < live_count)[:, None], attended, jnp.zeros((), jnp.bfloat16)
    )
    mixed_rows = (
        reordered.astype(jnp.float32)
        + jnp.dot(attended, proj_weight, preferred_element_type=jnp.float32)
    ).astype(jnp.bfloat16)
    normed_two = layer_norm(mixed_rows.astype(jnp.float32), norm2_gain).astype(jnp.bfloat16)
    hidden = jax.nn.gelu(
        jnp.dot(normed_two, fc1_weight, preferred_element_type=jnp.float32), approximate=False
    ).astype(jnp.bfloat16)
    block_out = (
        mixed_rows.astype(jnp.float32)
        + jnp.dot(hidden, fc2_weight, preferred_element_type=jnp.float32)
    ).astype(jnp.bfloat16)
    return block_out.reshape(1, 1, row_count, feat_width)


def solution(mesh):
    placed = (
        P("gx", "gy", None, None),
        P("gx", "gy", None, None),
        P("gx", "gy"),
        P("gx", "gy", None),
        P(),
        P(),
        P(),
        P(),
        P(),
        P(),
        P(),
        P(),
        P(),
    )
    return jax.shard_map(
        per_device, mesh=mesh, in_specs=placed, out_specs=P("gx", "gy", None, None), check_vma=False
    )
```

profile of v0, /device:TPU:24, one launch (start us, length us, event | category | flops | bytes accessed | tf_op | source)
XLA Modules:
  0.0 786.1 jit_solution(5097755933025162668)
XLA Ops:
  1.6 1.0 scatter_custom_fusion
  3.4 10.7 %all-to-all-start = ((s32[128,1,1]{2,1,0:T(1,128)}), s32[128,1,1]{2,1,0:T(1,128)}, u32[]{:S(2)}, u32[]{:S(2)}) async-start(s32[128,1,1]{2,1,0:T(1,128)} %copy.103), calls=%async_computation | async-start | bytes 131072 | tf_op jit(solution)/shard_map/all_to_all | solution.py:107
  14.1 1.7 compare_and_fusion
  15.8 1.2 compare_select_fusion
  17.7 2.3 copy.104
  20.0 2.3 concatenate.21.clone
  22.2 222.0 %gather_fusion = bf16[55296,256]{1,0:T(8,128)(2,1)} fusion(bf16[2049,256]{1,0:T(8,128)(2,1)} %concatenate.21.clone, s32[55296]{0:T(1024)} %broadcast_clamp_fusion), kind=kCustom, calls=%fused_computation | custom fusion | bytes 56844288 | tf_op jit(solution)/shard_map/jit(_take)/gather | solution.py:84
  244.3 14.6 %fusion.71.clone.1.clone.4 = bf16[2048,256]{1,0:T(8,128)(2,1)S(1)} fusion(bf16[27,256,256]{2,1,0:T(8,128)(2,1)S(1)} %copy-done, bf16[27,2048,256]{2,1,0:T(8,128)(2,1)} %bitcast.139, pred[27,2048]{1,0:T(8,128)(4,1)} %compare_and_fusion), kind=kOutput, calls=%fused_computation.97.clone.clone.clone.clone.clone.1 | convolution fusion | flops 7262437376 | bytes 32954368 | tf_op jit(solution)/shard_map/dot_general | solution.py:85
  261.2 2.3 scatter_custom_fusion.1
  264.1 1.4 reduce.1
  265.5 1.6 reshape.386
  267.1 9.8 %all-to-all-start.1 = ((bf16[128,2,2048]{2,1,0:T(2,128)(2,1)}), bf16[128,2,2048]{2,1,0:T(2,128)(2,1)S(1)}, u32[]{:S(2)}, u32[]{:S(2)}) async-start(bf16[128,2,2048]{2,1,0:T(2,128)(2,1)} %reshape.386), calls=%async_computation.1 | async-start | bytes 2097152 | tf_op jit(solution)/shard_map/all_to_all | solution.py:106
  277.6 69.9 %all-reduce.2 = (s32[128]{0:T(128)S(1)}, s32[]{:T(128)}) all-reduce(s32[128]{0:T(128)S(1)} %bitcast_dynamic-update-slice_fusion, s32[]{:T(128)} %bitcast.13), channel_id=1, replica_groups=mesh['gx'=16,'gy'=8] {'gx','gy'}, use_global_device_ids=true, to_apply=%add.1 | all-reduce | flops 129 | bytes 1032
  347.5 3.2 reduce
  350.7 1.1 reshape.387
  351.8 3.4 scatter_custom_fusion.2
  356.7 1.5 convolution_convert_fusion
  358.2 1.7 copy-done.2
  360.1 1.3 copy-done.3
  361.4 1.2 constant_dynamic-slice_fusion.7
  362.6 1.9 collective-permute-start
  364.5 170.4 %while.13 = (s32[]{:T(128)}, s32[1]{0:T(128)}, s32[]{:T(128)}, s32[128,1]{0,1:T(1,128)S(1)}, s32[]{:T(128)}) while((s32[]{:T(128)}, s32[1]{0:T(128)}, s32[]{:T(128)}, s32[128,1]{0,1:T(1,128)S(1)}, s32[]{:T(128)}) %tuple.58), condition=%wide.region_8.9_spmd, body=%wide.region_7.8_spmd.sunk | while | flops 5 | bytes 107 | solution.py:19
  536.3 2.3 slice.106
  538.6 1.3 slice.107
  539.9 6.4 collective-permute-start.1
  546.6 1.1 fusion.180
  547.6 1.8 copy.132
  549.5 1.8 copy.129
  554.8 4.4 maximum_maximum_fusion
  559.2 8.8 %collective-permute-done.1 = bf16[1024,512]{1,0:T(8,128)(2,1)} collective-permute-done((bf16[1024,512]{1,0:T(8,128)(2,1)}, bf16[1024,512]{1,0:T(8,128)(2,1)}, u32[]{:S(2)}, u32[]{:S(2)}) %collective-permute-start.1) | collective-permute-done | bytes 1048608 | tf_op jit(solution)/shard_map/ppermute | solution.py:25
  568.0 6.5 dynamic_update_slice.3
  574.5 3.1 fusion.179
  583.6 18.8 %fusion.190 = (f32[8,1024]{1,0:T(8,128)S(1)}, f32[8,1024,1024]{1,2,0:T(8,128)}) fusion(pred[1024]{0:T(1024)(128)(4,1)S(1)} %get-tuple-element.113, bf16[1024,8,16]{0,2,1:T(8,128)(2,1)} %bitcast.149, bf16[1024,8,16]{0,2,1:T(8,128)(2,1)} %bitcast.161), kind=kOutput, calls=%fused_computation.239 | convolution fusion | flops 301990912 | bytes 34112512 | tf_op jit(solution)/shard_map/sub | solution.py:52
  602.4 15.8 %fusion.189 = (f32[8,1024]{1,0:T(8,128)S(1)}, f32[8,1024,1024]{1,2,0:T(8,128)}) fusion(pred[1024]{0:T(1024)(128)(4,1)S(1)} %get-tuple-element.113, bf16[1024,8,16]{0,2,1:T(8,128)(2,1)S(1)} %bitcast.148, bf16[1024,8,16]{0,2,1:T(8,128)(2,1)S(1)} %bitcast.160), kind=kOutput, calls=%fused_computation.238 | convolution fusion | flops 301990912 | bytes 34112512 | tf_op jit(solution)/shard_map/sub | solution.py:52
  618.1 15.6 %fusion.188 = (f32[8,1024]{1,0:T(8,128)S(1)}, f32[8,1024,1024]{1,2,0:T(8,128)}) fusion(pred[1024]{0:T(1024)(128)(4,1)S(1)} %get-tuple-element.114, bf16[1024,8,16]{0,2,1:T(8,128)(2,1)S(1)} %bitcast.147, bf16[1024,8,16]{0,2,1:T(8,128)(2,1)S(1)} %bitcast.159), kind=kOutput, calls=%fused_computation.237 | convolution fusion | flops 301990912 | bytes 34112512 | tf_op jit(solution)/shard_map/sub | solution.py:52
  633.7 15.5 %fusion.187 = (f32[8,1024]{1,0:T(8,128)S(1)}, f32[8,1024,1024]{1,2,0:T(8,128)}) fusion(pred[1024]{0:T(1024)(128)(4,1)S(1)} %get-tuple-element.114, bf16[1024,8,16]{0,2,1:T(8,128)(2,1)S(1)} %bitcast.146, bf16[1024,8,16]{0,2,1:T(8,128)(2,1)S(1)} %bitcast.158), kind=kOutput, calls=%fused_computation.236 | convolution fusion | flops 301990912 | bytes 34112512 | tf_op jit(solution)/shard_map/sub | solution.py:52
  649.3 15.8 %fusion.186 = (f32[8,1024]{1,0:T(8,128)S(1)}, f32[8,1024,1024]{1,2,0:T(8,128)}) fusion(pred[1024]{0:T(1024)(128)(4,1)S(1)} %get-tuple-element.115, bf16[1024,8,16]{0,2,1:T(8,128)(2,1)S(1)} %bitcast.145, bf16[1024,8,16]{0,2,1:T(8,128)(2,1)S(1)} %bitcast.157), kind=kOutput, calls=%fused_computation.235 | convolution fusion | flops 301990912 | bytes 34112512 | tf_op jit(solution)/shard_map/sub | solution.py:52
  665.1 16.2 %fusion.185 = (f32[8,1024]{1,0:T(8,128)}, f32[8,1024,1024]{1,2,0:T(8,128)}) fusion(pred[1024]{0:T(1024)(128)(4,1)S(1)} %get-tuple-element.115, bf16[1024,8,16]{0,2,1:T(8,128)(2,1)S(1)} %bitcast.144, bf16[1024,8,16]{0,2,1:T(8,128)(2,1)S(1)} %bitcast.156), kind=kOutput, calls=%fused_computation.234 | convolution fusion | flops 301990912 | bytes 34112512 | tf_op jit(solution)/shard_map/sub | solution.py:52
  681.3 12.5 %fusion.88 = bf16[8,16,1024]{2,1,0:T(8,128)(2,1)} fusion(bf16[1024,8,16]{0,2,1:T(8,128)(2,1)S(1)} %bitcast.155, f32[8,1024,1024]{1,2,0:T(8,128)} %get-tuple-element.129, f32[8,1024]{1,0:T(8,128)S(1)} %get-tuple-element.128), kind=kOutput, calls=%fused_computation.118 | convolution fusion | flops 285343744 | bytes 34111488 | tf_op jit(solution)/shard_map/hqk,khd->qhd/dot_general | solution.py:54
  693.8 11.9 %fusion.89 = bf16[8,16,1024]{2,1,0:T(8,128)(2,1)S(1)} fusion(bf16[1024,8,16]{0,2,1:T(8,128)(2,1)S(1)} %bitcast.154, f32[8,1024,1024]{1,2,0:T(8,128)} %get-tuple-element.127, f32[8,1024]{1,0:T(8,128)S(1)} %get-tuple-element.126), kind=kOutput, calls=%fused_computation.119 | convolution fusion | flops 285343744 | bytes 34111488 | tf_op jit(solution)/shard_map/hqk,khd->qhd/dot_general | solution.py:54
  705.7 11.9 %fusion.90 = bf16[8,16,1024]{2,1,0:T(8,128)(2,1)S(1)} fusion(bf16[1024,8,16]{0,2,1:T(8,128)(2,1)S(1)} %bitcast.153, f32[8,1024,1024]{1,2,0:T(8,128)} %get-tuple-element.125, f32[8,1024]{1,0:T(8,128)S(1)} %get-tuple-element.124), kind=kOutput, calls=%fused_computation.120 | convolution fusion | flops 285343744 | bytes 34111488 | tf_op jit(solution)/shard_map/hqk,khd->qhd/dot_general | solution.py:54
  717.6 11.9 %fusion.91 = bf16[8,16,1024]{2,1,0:T(8,128)(2,1)S(1)} fusion(bf16[1024,8,16]{0,2,1:T(8,128)(2,1)S(1)} %bitcast.152, f32[8,1024,1024]{1,2,0:T(8,128)} %get-tuple-element.123, f32[8,1024]{1,0:T(8,128)S(1)} %get-tuple-element.122), kind=kOutput, calls=%fused_computation.121 | convolution fusion | flops 285343744 | bytes 34111488 | tf_op jit(solution)/shard_map/hqk,khd->qhd/dot_general | solution.py:54
  729.5 11.8 %fusion.92 = bf16[8,16,1024]{2,1,0:T(8,128)(2,1)S(1)} fusion(bf16[1024,8,16]{0,2,1:T(8,128)(2,1)S(1)} %bitcast.150, f32[8,1024,1024]{1,2,0:T(8,128)} %get-tuple-element.121, f32[8,1024]{1,0:T(8,128)S(1)} %get-tuple-element.120), kind=kOutput, calls=%fused_computation.122 | convolution fusion | flops 285343744 | bytes 34111488 | tf_op jit(solution)/shard_map/hqk,khd->qhd/dot_general | solution.py:54
  741.4 12.5 %fusion.93 = bf16[8,16,1024]{2,1,0:T(8,128)(2,1)S(1)} fusion(bf16[1024,8,16]{0,2,1:T(8,128)(2,1)S(1)} %bitcast.151, f32[8,1024,1024]{1,2,0:T(8,128)} %get-tuple-element.119, f32[8,1024]{1,0:T(8,128)S(1)} %copy-done.23), kind=kOutput, calls=%fused_computation.123 | convolution fusion | flops 285343744 | bytes 34111488 | tf_op jit(solution)/shard_map/hqk,khd->qhd/dot_general | solution.py:54
  753.9 5.4 convert_reduce_fusion
  759.3 0.9 copy-done.6
  760.6 23.1 %fusion.80 = bf16[1,1,2048,256]{2,3,1,0:T(8,128)(2,1)} fusion(bf16[1024,256]{1,0:T(8,128)(2,1)} %param.27, bf16[256,1024]{1,0:T(8,128)(2,1)} %param.26, bf16[2048,256]{0,1:T(8,128)(2,1)} %copy-done.6, f32[256]{0:T(256)} %param.25, f32[2048]{0:T(1024)S(1)} %add_rsqrt_fusion, f32[2048]{0:T(1024)S(1)} %broadcast_multiply_fusion), kind=kOutput, calls=%fused_computation.102 | convolution fusion | flops 2287992832 | bytes 3163136 | tf_op jit(solution)/shard_map/dot_general | solution.py:172
  783.7 2.3 copy.134
  (223 shorter events, 101.1 us)
Async XLA Ops:
  0.0 244.2 %copy-start = (bf16[27,256,256]{2,1,0:T(8,128)(2,1)S(1)}, bf16[27,256,256]{2,1,0:T(8,128)(2,1)}, u32[]{:S(2)}) copy-start(bf16[27,256,256]{2,1,0:T(8,128)(2,1)} %param.19) | copy-start | bytes 10616836
  3.4 263.7 %all-to-all-start = ((s32[128,1,1]{2,1,0:T(1,128)}), s32[128,1,1]{2,1,0:T(1,128)}, u32[]{:S(2)}, u32[]{:S(2)}) async-start(s32[128,1,1]{2,1,0:T(1,128)} %copy.103), calls=%async_computation | async-start | bytes 131072 | tf_op jit(solution)/shard_map/all_to_all | solution.py:107
  244.2 14.6 %copy-start.17 = (bf16[256,256]{1,0:T(8,128)(2,1)S(1)}, bf16[256,256]{1,0:T(8,128)(2,1)}, u32[]{:S(2)}) copy-start(bf16[256,256]{1,0:T(8,128)(2,1)} %param.20) | copy-start | bytes 393220
  244.2 15.4 %copy-start.4 = (bf16[1,1,2048,256]{2,3,1,0:T(8,128)(2,1)S(1)}, bf16[1,1,2048,256]{2,3,1,0:T(8,128)(2,1)}, u32[]{:S(2)}) copy-start(bf16[1,1,2048,256]{2,3,1,0:T(8,128)(2,1)} %copy.104) | copy-start | bytes 3145732
  244.3 15.4 %copy-start.19 = (f32[256]{0:T(256)S(1)}, f32[256]{0:T(256)}, u32[]{:S(2)}) copy-start(f32[256]{0:T(256)} %param.21) | copy-start | bytes 3076
  267.1 89.6 %copy-start.7 = (bf16[256,768]{1,0:T(8,128)(2,1)S(1)}, bf16[256,768]{1,0:T(8,128)(2,1)}, u32[]{:S(2)}) copy-start(bf16[256,768]{1,0:T(8,128)(2,1)} %param.23) | copy-start | bytes 1179652
  267.1 89.6 %copy-start.20 = (f32[256]{0:T(256)S(1)}, f32[256]{0:T(256)}, u32[]{:S(2)}) copy-start(f32[256]{0:T(256)} %param.22) | copy-start | bytes 3076
  267.1 83.6 %all-to-all-start.1 = ((bf16[128,2,2048]{2,1,0:T(2,128)(2,1)}), bf16[128,2,2048]{2,1,0:T(2,128)(2,1)S(1)}, u32[]{:S(2)}, u32[]{:S(2)}) async-start(bf16[128,2,2048]{2,1,0:T(2,128)(2,1)} %reshape.386), calls=%async_computation.1 | async-start | bytes 2097152 | tf_op jit(solution)/shard_map/all_to_all | solution.py:106
  358.2 1.7 copy-start.2
  360.0 1.3 copy-start.3
  362.6 192.2 %collective-permute-start = (bf16[1024,512]{1,0:T(8,128)(2,1)}, bf16[1024,512]{1,0:T(8,128)(2,1)}, u32[]{:S(2)}, u32[]{:S(2)}) collective-permute-start(bf16[1024,512]{1,0:T(8,128)(2,1)} %constant_dynamic-slice_fusion.7), channel_id=1, source_target_pairs={{0,1},{1,2},{2,3},{3,4},{4,5},{5,6},{6,7},{7,8},{8,9},{9,10},{10,1... | collective-permute-start | bytes 3145736 | tf_op jit(solution)/shard_map/ppermute | solution.py:25
  539.9 28.1 %collective-permute-start.1 = (bf16[1024,512]{1,0:T(8,128)(2,1)}, bf16[1024,512]{1,0:T(8,128)(2,1)}, u32[]{:S(2)}, u32[]{:S(2)}) collective-permute-start(bf16[1024,512]{1,0:T(8,128)(2,1)} %slice.106), channel_id=1, source_target_pairs={{1,0},{2,1},{3,2},{4,3},{5,4},{6,5},{7,6},{8,7},{9,8},{10,9},{11,1... | collective-permute-start | bytes 3145736 | tf_op jit(solution)/shard_map/ppermute | solution.py:25
  583.6 18.8 %copy-start.11 = (bf16[1024,128]{0,1:T(8,128)(2,1)S(1)}, bf16[1024,128]{0,1:T(8,128)(2,1)}, u32[]{:S(2)}) copy-start(bf16[1024,128]{0,1:T(8,128)(2,1)} %copy.125) | copy-start | bytes 786436
  602.4 15.8 %copy-start.10 = (bf16[1024,128]{0,1:T(8,128)(2,1)S(1)}, bf16[1024,128]{0,1:T(8,128)(2,1)}, u32[]{:S(2)}) copy-start(bf16[1024,128]{0,1:T(8,128)(2,1)} %copy.121) | copy-start | bytes 786436
  618.1 15.6 %copy-start.9 = (bf16[1024,128]{0,1:T(8,128)(2,1)S(1)}, bf16[1024,128]{0,1:T(8,128)(2,1)}, u32[]{:S(2)}) copy-start(bf16[1024,128]{0,1:T(8,128)(2,1)} %copy.117) | copy-start | bytes 786436
  633.7 15.5 %copy-start.8 = (bf16[1024,128]{0,1:T(8,128)(2,1)S(1)}, bf16[1024,128]{0,1:T(8,128)(2,1)}, u32[]{:S(2)}) copy-start(bf16[1024,128]{0,1:T(8,128)(2,1)} %copy.113) | copy-start | bytes 786436
  681.3 12.6 %copy-start.16 = (bf16[1024,128]{0,1:T(8,128)(2,1)S(1)}, bf16[1024,128]{0,1:T(8,128)(2,1)}, u32[]{:S(2)}) copy-start(bf16[1024,128]{0,1:T(8,128)(2,1)} %copy.124) | copy-start | bytes 786436
  693.8 11.9 %copy-start.15 = (bf16[1024,128]{0,1:T(8,128)(2,1)S(1)}, bf16[1024,128]{0,1:T(8,128)(2,1)}, u32[]{:S(2)}) copy-start(bf16[1024,128]{0,1:T(8,128)(2,1)} %copy.120) | copy-start | bytes 786436
  705.7 11.9 %copy-start.14 = (bf16[1024,128]{0,1:T(8,128)(2,1)S(1)}, bf16[1024,128]{0,1:T(8,128)(2,1)}, u32[]{:S(2)}) copy-start(bf16[1024,128]{0,1:T(8,128)(2,1)} %copy.116) | copy-start | bytes 786436
  717.6 11.9 %copy-start.12 = (bf16[1024,128]{0,1:T(8,128)(2,1)S(1)}, bf16[1024,128]{0,1:T(8,128)(2,1)}, u32[]{:S(2)}) copy-start(bf16[1024,128]{0,1:T(8,128)(2,1)} %copy.112) | copy-start | bytes 786436
  729.5 11.9 %copy-start.13 = (bf16[1024,128]{0,1:T(8,128)(2,1)S(1)}, bf16[1024,128]{0,1:T(8,128)(2,1)}, u32[]{:S(2)}) copy-start(bf16[1024,128]{0,1:T(8,128)(2,1)} %copy.108) | copy-start | bytes 786436
  729.5 11.9 %copy-start.23 = (f32[8,1024]{1,0:T(8,128)S(1)}, f32[8,1024]{1,0:T(8,128)}, u32[]{:S(2)}) copy-start(f32[8,1024]{1,0:T(8,128)} %get-tuple-element.118) | copy-start | bytes 98308
  741.4 12.5 %copy-start.5 = (f32[2048,256]{0,1:T(8,128)S(1)}, f32[2048,256]{0,1:T(8,128)}, u32[]{:S(2)}) copy-start(f32[2048,256]{0,1:T(8,128)} %copy.132) | copy-start | bytes 6291460
  741.4 12.5 %copy-start.18 = (pred[2048]{0:T(1024)(128)(4,1)S(1)}, pred[2048]{0:T(1024)(128)(4,1)}, u32[]{:S(2)}) copy-start(pred[2048]{0:T(1024)(128)(4,1)} %iota_compare_fusion.1) | copy-start | bytes 6148
  741.4 12.5 %copy-start.21 = (bf16[256,256]{1,0:T(8,128)(2,1)S(1)}, bf16[256,256]{1,0:T(8,128)(2,1)}, u32[]{:S(2)}) copy-start(bf16[256,256]{1,0:T(8,128)(2,1)} %param.24) | copy-start | bytes 393220
  741.4 12.5 %copy-start.22 = (bf16[8,16,1024]{2,1,0:T(8,128)(2,1)S(1)}, bf16[8,16,1024]{2,1,0:T(8,128)(2,1)}, u32[]{:S(2)}) copy-start(bf16[8,16,1024]{2,1,0:T(8,128)(2,1)} %fusion.88) | copy-start | bytes 786436
  759.3 1.0 copy-start.6
  760.6 25.3 %copy-start.1 = (bf16[27,256,256]{2,1,0:T(8,128)(2,1)S(1)}, bf16[27,256,256]{2,1,0:T(8,128)(2,1)}, u32[]{:S(2)}) copy-start(bf16[27,256,256]{2,1,0:T(8,128)(2,1)} %param.19) | copy-start | bytes 10616836
where the time goes:
time: 800 us; the launch traced here: 786 us
  local copies, waits for them, and re-layouts  356 us (44%)
  matrix products  215 us (27%)
  loops' own time  88.4 us (11%)
  blocking collectives  69.9 us (9%)
  starting transfers between devices  28.8 us (4%)
  other arithmetic  17.8 us (2%)
  waiting for transfers between devices  8.76 us (1%)
    gather x1, local copies, waits for them, and re-layouts, per_device(): jnp.take(padded, tap_rows, axis=0).reshape(tap_count, row_count, feat_width)  222 us
    sub x6, matrix products, attend_patch(): exp_scores = jnp.exp(scores - row_max)  97.7 us
    another operation x1, loops' own time, entering(): return lax.fori_loop(0, count - 1, hop, so_far)  88.4 us
    dynamic_slice x127, local copies, waits for them, and re-layouts, hop(): longer = join(so_far, pieces[position])  82 us
    dot_general x6, matrix products, attend_patch(): jnp.einsum('hqk,khd->qhd', weights, v_part, preferred_element_type=jnp.fl...  72.4 us
    unnamed x1, blocking collectives  69.9 us
    dot_general x1, matrix products, per_device(): jnp.dot(hidden, fc2_weight, preferred_element_type=jnp.float32)  23.1 us
  transfers between devices with their start and end apart: 4, of which 1 were waited for; matrix products, arithmetic and copies ran while one was open for 45% of the time, Pallas kernels for 0%

commit v1 on v0

v1 whole, which is shorter than its diff:
```python
import functools

import jax
import jax.numpy as jnp
from jax import lax
from jax.experimental import pallas as pl
from jax.experimental.pallas import tpu as pltpu
from jax.sharding import PartitionSpec as P

HEADS = 16
PATCH = 1024
BLOCK = 16
SUPER = 512
TILE = 128
WINDOW = 256
QTILE = 256
LANES = 128
AXES = ("gx", "gy")


def normalised(values, gain):
    centre = values - jnp.mean(values, axis=-1, keepdims=True)
    spread = jnp.mean(centre * centre, axis=-1, keepdims=True)
    return centre * lax.rsqrt(spread + 1e-05) * gain


def put(ref, start, value):
    for half in range(ref.shape[0]):
        ref[half, pl.ds(start, value.shape[0]), :] = value[:, half * LANES : (half + 1) * LANES]


def get(ref, start, size):
    return jnp.concatenate([ref[half, pl.ds(start, size), :] for half in range(ref.shape[0])], axis=1)


def conv_kernel(dest_ref, taps_ref, rows_ref, weight_ref, cpe_ref, gain_ref, out_ref, picked_ref):
    taps, span = taps_ref.shape
    total, width = rows_ref.shape
    step = pl.program_id(0)
    lanes = lax.broadcasted_iota(jnp.int32, (TILE, WINDOW), 1)

    for part in range(span // TILE):
        chunk = taps_ref[:, part * TILE : (part + 1) * TILE]
        as_float = chunk.astype(jnp.float32)
        low = jnp.min(as_float).astype(jnp.int32)
        high = jnp.max(jnp.where(chunk < total, as_float, -1.0)).astype(jnp.int32)
        low = low // BLOCK * BLOCK
        passes = (high - low + WINDOW) // WINDOW
        low = jnp.minimum(low, total - passes * WINDOW)
        filled = jnp.concatenate(
            [chunk, jnp.full((-taps % 8, TILE), total, jnp.int32)], axis=0
        )
        columns = filled.T
        here = pl.ds(part * TILE, TILE)

        def pick(start):
            window = rows_ref[pl.ds(pl.multiple_of(start, BLOCK), WINDOW), :]
            shifted = columns - start
            hot = jnp.concatenate(
                [
                    jnp.where(shifted[:, tap : tap + 1] == lanes, 1.0, 0.0).astype(jnp.bfloat16)
                    for tap in range(taps)
                ],
                axis=0,
            )
            return jnp.dot(hot, window, preferred_element_type=jnp.float32).astype(jnp.bfloat16)

        first = pick(low)
        for tap in range(taps):
            picked_ref[here, tap * width : (tap + 1) * width] = first[tap * TILE : (tap + 1) * TILE]

        @pl.loop(1, passes)
        def _(index):
            more = pick(low + index * WINDOW)
            for tap in range(taps):
                columns_here = slice(tap * width, (tap + 1) * width)
                picked_ref[here, columns_here] += more[tap * TILE : (tap + 1) * TILE]

    summed = jnp.dot(picked_ref[...], weight_ref[...], preferred_element_type=jnp.float32)
    linear = jnp.dot(
        summed.astype(jnp.bfloat16), cpe_ref[...], preferred_element_type=jnp.float32
    )
    own = rows_ref[pl.ds(pl.multiple_of(step * span, span), span), :].astype(jnp.float32)
    encoded = (own + normalised(linear, gain_ref[...])).astype(jnp.bfloat16)
    for block in range(span // BLOCK):
        place = dest_ref[step * (span // BLOCK) + block]
        out_ref[place] = encoded[block * BLOCK : (block + 1) * BLOCK]


def convolved(features, neighbours, dest, conv_weight, cpe_weight, cpe_gain):
    total, width = features.shape
    taps = neighbours.shape[0]
    blocks = total // BLOCK
    whole = lambda step, *_: (0, 0)
    return pl.pallas_call(
        conv_kernel,
        out_shape=jax.ShapeDtypeStruct((blocks, BLOCK, width), jnp.bfloat16),
        grid_spec=pltpu.PrefetchScalarGridSpec(
            num_scalar_prefetch=1,
            grid=(total // SUPER,),
            in_specs=[
                pl.BlockSpec((taps, SUPER), lambda step, *_: (0, step)),
                pl.BlockSpec((total, width), whole),
                pl.BlockSpec((taps * width, width), whole),
                pl.BlockSpec((width, width), whole),
                pl.BlockSpec((1, width), whole),
            ],
            out_specs=pl.BlockSpec((blocks, BLOCK, width), lambda step, *_: (0, 0, 0)),
            scratch_shapes=[pltpu.VMEM((SUPER, taps * width), jnp.bfloat16)],
        ),
        compiler_params=pltpu.CompilerParams(vmem_limit_bytes=56 << 20),
        name="convolve",
    )(dest, neighbours, features, conv_weight, cpe_weight, cpe_gain)


def place_kernel(slots_ref, count_ref, arrived_ref, moved_ref, tail_ref, wide_ref):
    blocks = arrived_ref.shape[0]

    @pl.loop(0, blocks)
    def _(source):
        row = pl.multiple_of(slots_ref[source] * BLOCK, BLOCK)
        block = arrived_ref[source]
        moved_ref[pl.ds(row, BLOCK), :] = block
        put(wide_ref, row, block.astype(jnp.float32))

    start = count_ref[0] - PATCH
    for part in range(PATCH // QTILE):
        tail_ref[part * QTILE : (part + 1) * QTILE, :] = get(
            wide_ref, start + part * QTILE, QTILE
        ).astype(jnp.bfloat16)


def placed_rows(slots, count, arrived):
    blocks, block, width = arrived.shape
    vmem = pl.BlockSpec(memory_space=pltpu.VMEM)
    smem = pl.BlockSpec(memory_space=pltpu.SMEM)
    return pl.pallas_call(
        place_kernel,
        out_shape=(
            jax.ShapeDtypeStruct((blocks * block, width), jnp.bfloat16),
            jax.ShapeDtypeStruct((PATCH, width), jnp.bfloat16),
        ),
        in_specs=[smem, smem, vmem],
        out_specs=(vmem, vmem),
        scratch_shapes=[pltpu.VMEM((width // LANES, blocks * block, LANES), jnp.float32)],
        compiler_params=pltpu.CompilerParams(vmem_limit_bytes=32 << 20),
        name="place",
    )(slots, count, arrived)


def block_kernel(
    scalars_ref,
    moved_ref,
    tail_ref,
    head_ref,
    gain_one_ref,
    qkv_ref,
    proj_ref,
    gain_two_ref,
    fc_one_ref,
    fc_two_ref,
    out_ref,
    source_ref,
    own_ref,
    keys_ref,
    values_ref,
    result_ref,
    gathered_ref,
):
    rows, width = moved_ref.shape
    skew = scalars_ref[0]
    live = scalars_ref[1]
    known = scalars_ref[2]
    live_end = skew + live

    for part in range(PATCH // QTILE):
        piece = tail_ref[part * QTILE : (part + 1) * QTILE, :].astype(jnp.float32)
        put(source_ref, skew + part * QTILE, piece)
    for part in range(rows // QTILE):
        piece = moved_ref[part * QTILE : (part + 1) * QTILE, :].astype(jnp.float32)
        put(source_ref, PATCH + skew + part * QTILE, piece)
        put(own_ref, skew + part * QTILE, piece)
    for part in range(PATCH // QTILE):
        piece = head_ref[part * QTILE : (part + 1) * QTILE, :].astype(jnp.float32)
        put(source_ref, PATCH + live_end + part * QTILE, piece)

    per_patch = PATCH // QTILE
    patches = (live_end + PATCH - 1) // PATCH

    @pl.loop(0, patches)
    def _(patch):
        for part in range(per_patch):
            start = pl.multiple_of(PATCH + patch * PATCH + part * QTILE, QTILE)
            normed = normalised(get(source_ref, start, QTILE), gain_one_ref[...])
            pair = jnp.dot(
                normed.astype(jnp.bfloat16),
                qkv_ref[:, width:],
                preferred_element_type=jnp.float32,
            )
            columns = slice(part * QTILE, (part + 1) * QTILE)
            keys_ref[patch, :, columns] = pair[:, :width].T.astype(jnp.bfloat16)
            values_ref[patch, columns, :] = pair[:, width:].astype(jnp.bfloat16)

    head_of_lane = lax.broadcasted_iota(jnp.int32, (QTILE, width), 1) // (width // HEADS)

    @pl.loop(skew // QTILE, (skew + rows + QTILE - 1) // QTILE)
    def _(tile):
        start = pl.multiple_of(tile * QTILE, QTILE)
        here = get(own_ref, start, QTILE)
        gathered_ref[...] = jnp.zeros((QTILE, width), jnp.float32)

        @pl.when(start < live_end)
        def _():
            patch = tile // per_patch
            normed = normalised(here, gain_one_ref[...]).astype(jnp.bfloat16)
            queries = jnp.dot(normed, qkv_ref[:, :width], preferred_element_type=jnp.float32)
            queries = queries.astype(jnp.bfloat16) * jnp.bfloat16((width // HEADS) ** -0.5)
            spot = patch * PATCH + lax.broadcasted_iota(jnp.int32, (1, PATCH), 1)
            bias = jnp.where(spot < known, 0.0, -1e30)

            @pl.loop(0, HEADS)
            def _(head):
                mine = head_of_lane == head
                one = jnp.where(mine, queries, jnp.bfloat16(0))
                scores = jnp.dot(one, keys_ref[patch], preferred_element_type=jnp.float32) + bias
                top = jnp.max(scores, axis=-1, keepdims=True)
                grown = jnp.exp(scores - top)
                share = jnp.sum(grown, axis=-1, keepdims=True)
                mixed = jnp.dot(
                    grown.astype(jnp.bfloat16), values_ref[patch], preferred_element_type=jnp.float32
                )
                gathered_ref[...] = jnp.where(mine, mixed / share, gathered_ref[...])

        spots = start + lax.broadcasted_iota(jnp.int32, (QTILE, 1), 0)
        attended = jnp.where(spots < live_end, gathered_ref[...], 0.0)
        projected = jnp.dot(
            attended.astype(jnp.bfloat16), proj_ref[...], preferred_element_type=jnp.float32
        )
        mixed = (here + projected).astype(jnp.bfloat16).astype(jnp.float32)
        normed = normalised(mixed, gain_two_ref[...]).astype(jnp.bfloat16)
        hidden = jnp.dot(normed, fc_one_ref[...], preferred_element_type=jnp.float32)
        hidden = 0.5 * hidden * (1.0 + lax.erf(hidden * 0.5**0.5))
        final = mixed + jnp.dot(
            hidden.astype(jnp.bfloat16), fc_two_ref[...], preferred_element_type=jnp.float32
        )
        put(result_ref, start, final)

    for part in range(rows // QTILE):
        out_ref[part * QTILE : (part + 1) * QTILE, :] = get(
            result_ref, skew + part * QTILE, QTILE
        ).astype(jnp.bfloat16)


def finished(scalars, moved, tail, head, gain_one, qkv, proj, gain_two, fc_one, fc_two):
    rows, width = moved.shape
    vmem = pl.BlockSpec(memory_space=pltpu.VMEM)
    smem = pl.BlockSpec(memory_space=pltpu.SMEM)
    most = rows // PATCH + 1
    halves = width // LANES
    return pl.pallas_call(
        block_kernel,
        out_shape=jax.ShapeDtypeStruct((rows, width), jnp.bfloat16),
        in_specs=[smem] + [vmem] * 9,
        out_specs=vmem,
        scratch_shapes=[
            pltpu.VMEM((halves, (most + 2) * PATCH, LANES), jnp.float32),
            pltpu.VMEM((halves, most * PATCH, LANES), jnp.float32),
            pltpu.VMEM((most, width, PATCH), jnp.bfloat16),
            pltpu.VMEM((most, PATCH, width), jnp.bfloat16),
            pltpu.VMEM((halves, most * PATCH, LANES), jnp.float32),
            pltpu.VMEM((QTILE, width), jnp.float32),
        ],
        compiler_params=pltpu.CompilerParams(vmem_limit_bytes=56 << 20),
        name="attend",
    )(scalars, moved, tail, head, gain_one, qkv, proj, gain_two, fc_one, fc_two)


def passed_along(shard, by):
    count = lax.axis_size(AXES)
    pairs = [(i, i + by) for i in range(count) if 0 <= i + by < count]
    return lax.ppermute(shard, AXES, pairs)


def per_device(
    features,
    neighbours,
    counts,
    block_dest,
    conv_weight,
    cpe_weight,
    cpe_gain,
    norm1_gain,
    qkv_weight,
    proj_weight,
    norm2_gain,
    fc1_weight,
    fc2_weight,
):
    rows, width = features.shape[2:]
    taps = neighbours.shape[2]
    blocks = block_dest.shape[2]
    devices = lax.axis_size(AXES)
    me = lax.axis_index(AXES)
    own_count = counts.reshape(1)
    place = block_dest.reshape(blocks)
    target = place // blocks
    label = jnp.stack([place % blocks, jnp.broadcast_to(own_count, (blocks,))], axis=1)
    labels = jnp.zeros((devices, 2), jnp.int32).at[target].set(label)
    labels = lax.all_to_all(labels, AXES, split_axis=0, concat_axis=0, tiled=True)
    slots, every_count = labels[:, 0], labels[:, 1]
    outgoing = convolved(
        features.reshape(rows, width),
        neighbours.reshape(taps, rows),
        target,
        conv_weight.reshape(taps * width, width),
        cpe_weight,
        cpe_gain.reshape(1, width),
    )
    arrived = lax.all_to_all(outgoing, AXES, split_axis=0, concat_axis=0, tiled=True)
    moved, tail = placed_rows(slots, own_count, arrived)
    before = passed_along(tail, 1)
    after = passed_along(moved[:PATCH], -1)
    earlier = jnp.arange(devices) < me
    offset = jnp.sum(jnp.where(earlier, every_count, 0))
    known = jnp.sum(jnp.where(earlier, 0, every_count))
    skew = offset % PATCH
    scalars = jnp.stack([skew, own_count[0], known + skew])
    block_out = finished(
        scalars,
        moved,
        before,
        after,
        norm1_gain.reshape(1, width),
        qkv_weight,
        proj_weight,
        norm2_gain.reshape(1, width),
        fc1_weight,
        fc2_weight,
    )
    return block_out.reshape(1, 1, rows, width)


def solution(mesh):
    placed = (
        P("gx", "gy", None, None),
        P("gx", "gy", None, None),
        P("gx", "gy"),
        P("gx", "gy", None),
    ) + (P(),) * 9
    return jax.shard_map(
        per_device, mesh=mesh, in_specs=placed, out_specs=P("gx", "gy", None, None), check_vma=False
    )
```

time: 800 us -> 242 us (0.30)
  the two profiles are of different devices: /device:TPU:24 before, /device:TPU:19 now
where the time goes in v1:
time: 242 us; the launch traced here: 241 us
  Pallas kernels  178 us (74%)
  starting transfers between devices  26.6 us (11%)
  waiting for transfers between devices  26.4 us (11%)
  local copies, waits for them, and re-layouts  4.29 us (2%)
  between operations  3.31 us (1%)
  other arithmetic  3.18 us (1%)
    pallas_call x1, Pallas kernels, finished(): pl.pallas_call(block_kernel, out_shape=jax.ShapeDtypeStruct((rows, width)...  147 us
    pallas_call x1, Pallas kernels, convolved(): pl.pallas_call(conv_kernel, out_shape=jax.ShapeDtypeStruct((blocks, BLOCK...  28.9 us
    all_to_all x1, waiting for transfers between devices, per_device(): lax.all_to_all(outgoing, AXES, split_axis=0, concat_axis=0, tiled=True)  16 us
    all_to_all x1, starting transfers between devices, per_device(): lax.all_to_all(labels, AXES, split_axis=0, concat_axis=0, tiled=True)  10.6 us
    ppermute x2, waiting for transfers between devices, passed_along(): return lax.ppermute(shard, AXES, pairs)  10.4 us
    all_to_all x1, starting transfers between devices, per_device(): lax.all_to_all(outgoing, AXES, split_axis=0, concat_axis=0, tiled=True)  9.76 us
    ppermute x2, starting transfers between devices, passed_along(): return lax.ppermute(shard, AXES, pairs)  6.18 us
  transfers between devices with their start and end apart: 4, of which 3 were waited for; matrix products, arithmetic and copies ran while one was open for 2% of the time, Pallas kernels for 12%

profile of v1, /device:TPU:19, one launch (start us, length us, event | category | flops | bytes accessed | tf_op | source)
XLA Modules:
  0.0 241.4 jit_solution(8572934393589253698)
XLA Ops:
  0.7 0.7 and_select_fusion.1
  1.3 0.1 copy.19
  1.4 1.4 scatter_custom_fusion
  2.9 10.6 %all-to-all-start = ((s32[128,1,2]{2,1,0:T(1,128)}), s32[128,1,2]{2,1,0:T(1,128)S(1)}, u32[]{:S(2)}, u32[]{:S(2)}) async-start(s32[128,1,2]{2,1,0:T(1,128)} %bitcast.4), calls=%async_computation | async-start | bytes 131072 | tf_op jit(solution)/shard_map/all_to_all | solution.py:309
  13.5 1.3 and_select_fusion.dest_ref
  14.8 1.7 copy.21
  16.5 28.9 %convolve.1 = bf16[128,16,256]{2,1,0:T(8,128)(2,1)} custom-call(s32[128]{0:T(128)} %and_select_fusion.dest_ref, s32[27,2048]{1,0:T(8,128)} %bitcast.50, bf16[2048,256]{1,0:T(8,128)(2,1)} %bitcast.49, bf16[6912,256]{1,0:T(8,128)(2,1)} %bitcast.48, bf16[256,256]{1,0:T(8,128)(2,1)} %cpe_ref.1, f32[1,256]{1,0:T(1,128)} %bitcast.54), custom_call_target="tpu_custom_call" | custom-call | tf_op jit(solution)/shard_map/convolve/pallas_call | solution.py:95
  45.4 0.0 all-to-all-done
  45.4 9.8 %all-to-all-start.1 = ((bf16[128,16,256]{2,1,0:T(8,128)(2,1)}), bf16[128,16,256]{2,1,0:T(8,128)(2,1)S(1)}, u32[]{:S(2)}, u32[]{:S(2)}) async-start(bf16[128,16,256]{2,1,0:T(8,128)(2,1)} %convolve.1), calls=%async_computation.1 | async-start | bytes 2097152 | tf_op jit(solution)/shard_map/all_to_all | solution.py:319
  55.1 0.2 slice_reduce_fusion
  55.3 16.0 %all-to-all-done.1.arrived_ref = bf16[128,16,256]{2,1,0:T(8,128)(2,1)S(1)} async-done(((bf16[128,16,256]{2,1,0:T(8,128)(2,1)}), bf16[128,16,256]{2,1,0:T(8,128)(2,1)S(1)}, u32[]{:S(2)}, u32[]{:S(2)}) %all-to-all-start.1) | async-done | bytes 1048608 | tf_op jit(solution)/shard_map/all_to_all | solution.py:319
  71.3 1.4 place.1
  72.7 0.0 copy-start
  72.8 4.3 %collective-permute-start.1 = (bf16[1024,256]{1,0:T(8,128)(2,1)S(1)}, bf16[1024,256]{1,0:T(8,128)(2,1)S(1)}, u32[]{:S(2)}, u32[]{:S(2)}) collective-permute-start(bf16[1024,256]{1,0:T(8,128)(2,1)S(1)} %slice.11), channel_id=1, source_target_pairs={{1,0},{2,1},{3,2},{4,3},{5,4},{6,5},{7,6},{8,7},{9,8},{10,9},{11,1... | collective-permute-start | bytes 1572872 | tf_op jit(solution)/shard_map/ppermute | solution.py:281
  77.1 1.9 collective-permute-start
  79.0 0.7 fusion.3
  82.2 0.6 pad_add_fusion.scalars_ref
  82.8 5.5 %collective-permute-done.1.head_ref = bf16[1024,256]{1,0:T(8,128)(2,1)S(1)} collective-permute-done((bf16[1024,256]{1,0:T(8,128)(2,1)S(1)}, bf16[1024,256]{1,0:T(8,128)(2,1)S(1)}, u32[]{:S(2)}, u32[]{:S(2)}) %collective-permute-start.1) | collective-permute-done | bytes 524320 | tf_op jit(solution)/shard_map/ppermute | solution.py:281
  88.4 0.0 copy-start.1
  88.4 4.9 %collective-permute-done.tail_ref = bf16[1024,256]{1,0:T(8,128)(2,1)S(1)} collective-permute-done((bf16[1024,256]{1,0:T(8,128)(2,1)S(1)}, bf16[1024,256]{1,0:T(8,128)(2,1)S(1)}, u32[]{:S(2)}, u32[]{:S(2)}) %collective-permute-start) | collective-permute-done | bytes 524320 | tf_op jit(solution)/shard_map/ppermute | solution.py:281
  93.3 0.0 copy-start.2
  93.3 0.0 copy-done
  93.3 0.0 copy-done.1
  93.3 0.8 copy-done.2
  94.1 147.4 %attend.1 = bf16[2048,256]{1,0:T(8,128)(2,1)} custom-call(s32[3]{0:T(128)} %pad_add_fusion.scalars_ref, bf16[2048,256]{1,0:T(8,128)(2,1)} %copy-done, bf16[1024,256]{1,0:T(8,128)(2,1)} %copy-done.2, bf16[1024,256]{1,0:T(8,128)(2,1)} %copy-done.1, f32[1,256]{1,0:T(1,128)} %bitcast.52, bf16[256,768]{1,0:T(8,128)(2,1)} %qkv_ref.1, bf16[256,256]{1,0:T(8,128)(2,1)} %proj_ref.1, ...), custom_call_target="tpu_custom_call" | custom-call | tf_op jit(solution)/shard_map/attend/pallas_call | solution.py:260
  (1 shorter events, 0.0 us)
Async XLA Ops:
  2.9 42.5 %all-to-all-start = ((s32[128,1,2]{2,1,0:T(1,128)}), s32[128,1,2]{2,1,0:T(1,128)S(1)}, u32[]{:S(2)}, u32[]{:S(2)}) async-start(s32[128,1,2]{2,1,0:T(1,128)} %bitcast.4), calls=%async_computation | async-start | bytes 131072 | tf_op jit(solution)/shard_map/all_to_all | solution.py:309
  45.4 26.0 %all-to-all-start.1 = ((bf16[128,16,256]{2,1,0:T(8,128)(2,1)}), bf16[128,16,256]{2,1,0:T(8,128)(2,1)S(1)}, u32[]{:S(2)}, u32[]{:S(2)}) async-start(bf16[128,16,256]{2,1,0:T(8,128)(2,1)} %convolve.1), calls=%async_computation.1 | async-start | bytes 2097152 | tf_op jit(solution)/shard_map/all_to_all | solution.py:319
  72.7 20.5 %copy-start = (bf16[2048,256]{1,0:T(8,128)(2,1)}, bf16[2048,256]{1,0:T(8,128)(2,1)S(1)}, u32[]{:S(2)}) copy-start(bf16[2048,256]{1,0:T(8,128)(2,1)S(1)} %get-tuple-element.7.moved_ref) | copy-start | bytes 3145732
  72.8 15.6 %collective-permute-start.1 = (bf16[1024,256]{1,0:T(8,128)(2,1)S(1)}, bf16[1024,256]{1,0:T(8,128)(2,1)S(1)}, u32[]{:S(2)}, u32[]{:S(2)}) collective-permute-start(bf16[1024,256]{1,0:T(8,128)(2,1)S(1)} %slice.11), channel_id=1, source_target_pairs={{1,0},{2,1},{3,2},{4,3},{5,4},{6,5},{7,6},{8,7},{9,8},{10,9},{11,1... | collective-permute-start | bytes 1572872 | tf_op jit(solution)/shard_map/ppermute | solution.py:281
  77.1 16.2 %collective-permute-start = (bf16[1024,256]{1,0:T(8,128)(2,1)S(1)}, bf16[1024,256]{1,0:T(8,128)(2,1)S(1)}, u32[]{:S(2)}, u32[]{:S(2)}) collective-permute-start(bf16[1024,256]{1,0:T(8,128)(2,1)S(1)} %get-tuple-element.8), channel_id=1, source_target_pairs={{0,1},{1,2},{2,3},{3,4},{4,5},{5,6},{6,7},{7,8},{8,9},{9,10},{10,1... | collective-permute-start | bytes 1572872 | tf_op jit(solution)/shard_map/ppermute | solution.py:281
  88.4 4.9 %copy-start.1 = (bf16[1024,256]{1,0:T(8,128)(2,1)}, bf16[1024,256]{1,0:T(8,128)(2,1)S(1)}, u32[]{:S(2)}) copy-start(bf16[1024,256]{1,0:T(8,128)(2,1)S(1)} %collective-permute-done.1.head_ref) | copy-start | bytes 1572868
  93.3 0.8 copy-start.2

commit v2 on v1

--- a/solution.py
+++ b/solution.py
@@ -1,5 +1,3 @@
-import functools
-
 import jax
 import jax.numpy as jnp
 from jax import lax
@@ -15,7 +13,8 @@
 WINDOW = 256
 QTILE = 256
 LANES = 128
-AXES = ("gx", "gy")
+SAFE_SCORE = 30.0
+SAFE_VALUE = 1e20
 
 
 def normalised(values, gain):
@@ -33,10 +32,23 @@
     return jnp.concatenate([ref[half, pl.ds(start, size), :] for half in range(ref.shape[0])], axis=1)
 
 
-def conv_kernel(dest_ref, taps_ref, rows_ref, weight_ref, cpe_ref, gain_ref, out_ref, picked_ref):
+def conv_kernel(
+    dest_ref,
+    count_ref,
+    taps_ref,
+    rows_ref,
+    weight_ref,
+    cpe_ref,
+    gain_ref,
+    out_ref,
+    notes_ref,
+    picked_ref,
+):
     taps, span = taps_ref.shape
     total, width = rows_ref.shape
+    blocks = out_ref.shape[0]
     step = pl.program_id(0)
+    note_lane = lax.broadcasted_iota(jnp.int32, (1, LANES), 1)
     lanes = lax.broadcasted_iota(jnp.int32, (TILE, WINDOW), 1)
 
     for part in range(span // TILE):
@@ -84,19 +96,24 @@
     encoded = (own + normalised(linear, gain_ref[...])).astype(jnp.bfloat16)
     for block in range(span // BLOCK):
         place = dest_ref[step * (span // BLOCK) + block]
-        out_ref[place] = encoded[block * BLOCK : (block + 1) * BLOCK]
-
-
-def convolved(features, neighbours, dest, conv_weight, cpe_weight, cpe_gain):
+        target, slot = place // blocks, place % blocks
+        out_ref[target] = encoded[block * BLOCK : (block + 1) * BLOCK]
+        notes_ref[target] = jnp.where(note_lane == 0, slot, count_ref[0])
+
+
+def convolved(features, neighbours, dest, count, conv_weight, cpe_weight, cpe_gain):
     total, width = features.shape
     taps = neighbours.shape[0]
     blocks = total // BLOCK
     whole = lambda step, *_: (0, 0)
     return pl.pallas_call(
         conv_kernel,
-        out_shape=jax.ShapeDtypeStruct((blocks, BLOCK, width), jnp.bfloat16),
+        out_shape=(
+            jax.ShapeDtypeStruct((blocks, BLOCK, width), jnp.bfloat16),
+            jax.ShapeDtypeStruct((blocks, 1, LANES), jnp.int32),
+        ),
         grid_spec=pltpu.PrefetchScalarGridSpec(
-            num_scalar_prefetch=1,
+            num_scalar_prefetch=2,
             grid=(total // SUPER,),
             in_specs=[
                 pl.BlockSpec((taps, SUPER), lambda step, *_: (0, step)),
@@ -105,51 +122,156 @@
                 pl.BlockSpec((width, width), whole),
                 pl.BlockSpec((1, width), whole),
             ],
-            out_specs=pl.BlockSpec((blocks, BLOCK, width), lambda step, *_: (0, 0, 0)),
+            out_specs=(
+                pl.BlockSpec((blocks, BLOCK, width), lambda step, *_: (0, 0, 0)),
+                pl.BlockSpec((blocks, 1, LANES), lambda step, *_: (0, 0, 0)),
+            ),
             scratch_shapes=[pltpu.VMEM((SUPER, taps * width), jnp.bfloat16)],
         ),
         compiler_params=pltpu.CompilerParams(vmem_limit_bytes=56 << 20),
         name="convolve",
-    )(dest, neighbours, features, conv_weight, cpe_weight, cpe_gain)
-
-
-def place_kernel(slots_ref, count_ref, arrived_ref, moved_ref, tail_ref, wide_ref):
-    blocks = arrived_ref.shape[0]
-
-    @pl.loop(0, blocks)
-    def _(source):
-        row = pl.multiple_of(slots_ref[source] * BLOCK, BLOCK)
-        block = arrived_ref[source]
+    )(dest, count, neighbours, features, conv_weight, cpe_weight, cpe_gain)
+
+
+def exchange_kernel(
+    count_ref,
+    outgoing_ref,
+    notes_ref,
+    moved_ref,
+    before_ref,
+    after_ref,
+    summary_ref,
+    arrived_ref,
+    heard_ref,
+    wide_ref,
+    tail_ref,
+    index_ref,
+    order_ref,
+    send_sem,
+    recv_sem,
+    note_send_sem,
+    note_recv_sem,
+    side_send_sem,
+    side_recv_sem,
+    local_sem,
+):
+    devices = outgoing_ref.shape[0]
+    across = lax.axis_size("gy")
+    me = lax.axis_index("gx") * across + lax.axis_index("gy")
+
+    def place_of(device):
+        return (device // across, device % across)
+
+    def to_peer(source, sink, sems, device):
+        return pltpu.make_async_remote_copy(
+            src_ref=source,
+            dst_ref=sink,
+            send_sem=sems[0],
+            recv_sem=sems[1],
+            device_id=place_of(device),
+            device_id_type=pl.DeviceIdType.MESH,
+        )
+
+    block_sems = (send_sem, recv_sem)
+    note_sems = (note_send_sem, note_recv_sem)
+
+    def send(step, _):
+        peer = (me + step) % devices
+        to_peer(notes_ref.at[peer], heard_ref.at[me], note_sems, peer).start()
+        to_peer(outgoing_ref.at[peer], arrived_ref.at[me], block_sems, peer).start()
+        return 0
+
+    lax.fori_loop(1, devices, send, 0)
+    arrived_ref[me] = outgoing_ref[me]
+    heard_ref[me] = notes_ref[me]
+    others = pl.ds(0, devices - 1)
+    all_notes = to_peer(notes_ref.at[others], heard_ref.at[others], note_sems, me)
+    all_notes.wait_recv()
+
+    heard = heard_ref[...].reshape(devices, LANES)
+    source = lax.broadcasted_iota(jnp.int32, (devices, LANES), 0)
+    lane = lax.broadcasted_iota(jnp.int32, (devices, LANES), 1)
+    slots = heard[:, :1]
+    index_ref[...] = jnp.max(jnp.where(slots == lane, source, 0), axis=0, keepdims=True)
+    counts = heard[:, 1:2]
+    offset = jnp.sum(jnp.where(source < me, counts, 0), axis=0, keepdims=True)
+    rest = jnp.sum(jnp.where(source < me, 0, counts), axis=0, keepdims=True)
+    summary_ref[...] = jnp.where(lane[:1] == 0, offset, rest)
+    order = pltpu.make_async_copy(index_ref, order_ref, local_sem)
+    order.start()
+    order.wait()
+
+    all_blocks = to_peer(outgoing_ref.at[others], arrived_ref.at[others], block_sems, me)
+    all_blocks.wait_recv()
+
+    def settle(slot, _):
+        block = arrived_ref[order_ref[0, slot]]
+        row = pl.multiple_of(slot * BLOCK, BLOCK)
         moved_ref[pl.ds(row, BLOCK), :] = block
         put(wide_ref, row, block.astype(jnp.float32))
-
-    start = count_ref[0] - PATCH
+        return 0
+
+    lax.fori_loop(0, devices, settle, 0)
+    following = (me + 1) % devices
+    previous = (me + devices - 1) % devices
+    head_sems = (side_send_sem.at[0], side_recv_sem.at[0])
+    tail_sems = (side_send_sem.at[1], side_recv_sem.at[1])
+    head = to_peer(moved_ref.at[pl.ds(0, PATCH)], after_ref, head_sems, previous)
+    head.start()
+    start = jnp.clip(count_ref[0] - PATCH, 0, moved_ref.shape[0] - PATCH)
     for part in range(PATCH // QTILE):
-        tail_ref[part * QTILE : (part + 1) * QTILE, :] = get(
-            wide_ref, start + part * QTILE, QTILE
-        ).astype(jnp.bfloat16)
-
-
-def placed_rows(slots, count, arrived):
-    blocks, block, width = arrived.shape
+        piece = get(wide_ref, start + part * QTILE, QTILE)
+        tail_ref[part * QTILE : (part + 1) * QTILE, :] = piece.astype(jnp.bfloat16)
+    tail = to_peer(tail_ref, before_ref, tail_sems, following)
+    tail.start()
+    all_notes.wait_send()
+    all_blocks.wait_send()
+    head.wait()
+    tail.wait()
+
+
+def exchanged(count, outgoing, notes):
+    blocks, block, width = outgoing.shape
+    rows = blocks * block
     vmem = pl.BlockSpec(memory_space=pltpu.VMEM)
     smem = pl.BlockSpec(memory_space=pltpu.SMEM)
+    side = jax.ShapeDtypeStruct((PATCH, width), jnp.bfloat16)
+    dma = pltpu.SemaphoreType.DMA
     return pl.pallas_call(
-        place_kernel,
+        exchange_kernel,
         out_shape=(
-            jax.ShapeDtypeStruct((blocks * block, width), jnp.bfloat16),
-            jax.ShapeDtypeStruct((PATCH, width), jnp.bfloat16),
+            jax.ShapeDtypeStruct((rows, width), jnp.bfloat16),
+            side,
+            side,
+            jax.ShapeDtypeStruct((1, LANES), jnp.int32),
         ),
-        in_specs=[smem, smem, vmem],
-        out_specs=(vmem, vmem),
-        scratch_shapes=[pltpu.VMEM((width // LANES, blocks * block, LANES), jnp.float32)],
-        compiler_params=pltpu.CompilerParams(vmem_limit_bytes=32 << 20),
-        name="place",
-    )(slots, count, arrived)
+        in_specs=[smem, vmem, vmem],
+        out_specs=(vmem, vmem, vmem, vmem),
+        scratch_shapes=[
+            pltpu.VMEM((blocks, block, width), jnp.bfloat16),
+            pltpu.VMEM((blocks, 1, LANES), jnp.int32),
+            pltpu.VMEM((width // LANES, rows, LANES), jnp.float32),
+            pltpu.VMEM((PATCH, width), jnp.bfloat16),
+            pltpu.VMEM((1, LANES), jnp.int32),
+            pltpu.SMEM((1, LANES), jnp.int32),
+            dma,
+            dma,
+            dma,
+            dma,
+            dma((2,)),
+            dma((2,)),
+            dma,
+        ],
+        compiler_params=pltpu.CompilerParams(
+            vmem_limit_bytes=32 << 20, has_side_effects=True
+        ),
+        name="exchange",
+    )(count, outgoing, notes)
 
 
 def block_kernel(
-    scalars_ref,
+    summary_ref,
+    count_ref,
     moved_ref,
     tail_ref,
     head_ref,
@@ -166,11 +288,13 @@
     values_ref,
     result_ref,
     gathered_ref,
+    reach_ref,
+    size_ref,
 ):
     rows, width = moved_ref.shape
-    skew = scalars_ref[0]
-    live = scalars_ref[1]
-    known = scalars_ref[2]
+    skew = summary_ref[0, 0] % PATCH
+    live = count_ref[0]
+    known = summary_ref[0, 1] + skew
     live_end = skew + live
 
     for part in range(PATCH // QTILE):
@@ -183,6 +307,18 @@
     for part in range(PATCH // QTILE):
         piece = head_ref[part * QTILE : (part + 1) * QTILE, :].astype(jnp.float32)
         put(source_ref, PATCH + live_end + part * QTILE, piece)
+
+    head_of_lane = lax.broadcasted_iota(jnp.int32, (QTILE, width), 1) // (width // HEADS)
+    left = lax.broadcasted_iota(jnp.int32, (width, width), 0) // (width // HEADS)
+    right = lax.broadcasted_iota(jnp.int32, (width, width), 1) // (width // HEADS)
+    same_head = jnp.where(left == right, 1.0, 0.0).astype(jnp.bfloat16)
+
+    def squares(values):
+        values = values.astype(jnp.float32)
+        total = jnp.dot(
+            (values * values).astype(jnp.bfloat16), same_head, preferred_element_type=jnp.float32
+        )
+        return 1.02 * total
 
     per_patch = PATCH // QTILE
     patches = (live_end + PATCH - 1) // PATCH
@@ -198,10 +334,18 @@
                 preferred_element_type=jnp.float32,
             )
             columns = slice(part * QTILE, (part + 1) * QTILE)
-            keys_ref[patch, :, columns] = pair[:, :width].T.astype(jnp.bfloat16)
-            values_ref[patch, columns, :] = pair[:, width:].astype(jnp.bfloat16)
-
-    head_of_lane = lax.broadcasted_iota(jnp.int32, (QTILE, width), 1) // (width // HEADS)
+            some_keys = pair[:, :width].astype(jnp.bfloat16).astype(jnp.float32)
+            keys_ref[patch, :, columns] = some_keys.T.astype(jnp.bfloat16)
+            alive = start - PATCH + lax.broadcasted_iota(jnp.int32, (QTILE, 1), 0) < known
+            some_values = pair[:, width:].astype(jnp.bfloat16)
+            for odd in range(2):
+                fitted = jnp.where(head_of_lane % 2 == odd, some_values, jnp.bfloat16(1))
+                values_ref[patch, odd, columns, :] = jnp.where(alive, fitted, jnp.bfloat16(0))
+            reach = jnp.max(squares(some_keys), axis=0, keepdims=True)
+            size = jnp.max(jnp.abs(pair[:, width:]), axis=0, keepdims=True)
+            reach_ref[patch] = reach if part == 0 else jnp.maximum(reach_ref[patch], reach)
+            size_ref[patch] = size if part == 0 else jnp.maximum(size_ref[patch], size)
+
 
     @pl.loop(skew // QTILE, (skew + rows + QTILE - 1) // QTILE)
     def _(tile):
@@ -215,21 +359,46 @@
             normed = normalised(here, gain_one_ref[...]).astype(jnp.bfloat16)
             queries = jnp.dot(normed, qkv_ref[:, :width], preferred_element_type=jnp.float32)
             queries = queries.astype(jnp.bfloat16) * jnp.bfloat16((width // HEADS) ** -0.5)
-            spot = patch * PATCH + lax.broadcasted_iota(jnp.int32, (1, PATCH), 1)
-            bias = jnp.where(spot < known, 0.0, -1e30)
-
-            @pl.loop(0, HEADS)
-            def _(head):
-                mine = head_of_lane == head
-                one = jnp.where(mine, queries, jnp.bfloat16(0))
-                scores = jnp.dot(one, keys_ref[patch], preferred_element_type=jnp.float32) + bias
-                top = jnp.max(scores, axis=-1, keepdims=True)
-                grown = jnp.exp(scores - top)
-                share = jnp.sum(grown, axis=-1, keepdims=True)
-                mixed = jnp.dot(
-                    grown.astype(jnp.bfloat16), values_ref[patch], preferred_element_type=jnp.float32
+            reach = jnp.max(squares(queries) * reach_ref[patch])
+            safe = (reach <= SAFE_SCORE**2) & (jnp.max(size_ref[patch]) <= SAFE_VALUE)
+
+            def gather(group, odd, softened):
+                heads = [2 * (group * 2 + index) + odd for index in range(2)]
+                one = jnp.concatenate(
+                    [jnp.where(head_of_lane == head, queries, jnp.bfloat16(0)) for head in heads],
+                    axis=0,
                 )
-                gathered_ref[...] = jnp.where(mine, mixed / share, gathered_ref[...])
+                scores = jnp.dot(one, keys_ref[patch], preferred_element_type=jnp.float32)
+                grown = softened(scores).astype(jnp.bfloat16)
+                mixed = jnp.dot(grown, values_ref[patch, odd], preferred_element_type=jnp.float32)
+                spare = LANES - 1 if odd == 0 else 0
+                mixed = mixed * (1.0 / mixed[:, spare : spare + 1])
+                so_far = gathered_ref[...]
+                for index, head in enumerate(heads):
+                    piece = mixed[index * QTILE : (index + 1) * QTILE]
+                    so_far = jnp.where(head_of_lane == head, piece, so_far)
+                gathered_ref[...] = so_far
+
+            @pl.when(safe)
+            def _():
+                @pl.loop(0, HEADS // 4, unroll=4)
+                def _(group):
+                    for odd in range(2):
+                        gather(group, odd, jnp.exp)
+
+            @pl.when(jnp.logical_not(safe))
+            def _():
+                spot = patch * PATCH + lax.broadcasted_iota(jnp.int32, (1, PATCH), 1)
+                bias = jnp.where(spot < known, 0.0, -1e30)
+
+                def softened(scores):
+                    scores = scores + bias
+                    return jnp.exp(scores - jnp.max(scores, axis=-1, keepdims=True))
+
+                @pl.loop(0, HEADS // 4)
+                def _(group):
+                    for odd in range(2):
+                        gather(group, odd, softened)
 
         spots = start + lax.broadcasted_iota(jnp.int32, (QTILE, 1), 0)
         attended = jnp.where(spots < live_end, gathered_ref[...], 0.0)
@@ -251,7 +420,7 @@
         ).astype(jnp.bfloat16)
 
 
-def finished(scalars, moved, tail, head, gain_one, qkv, proj, gain_two, fc_one, fc_two):
+def finished(summary, count, moved, tail, head, gain_one, qkv, proj, gain_two, fc_one, fc_two):
     rows, width = moved.shape
     vmem = pl.BlockSpec(memory_space=pltpu.VMEM)
     smem = pl.BlockSpec(memory_space=pltpu.SMEM)
@@ -260,25 +429,21 @@
     return pl.pallas_call(
         block_kernel,
         out_shape=jax.ShapeDtypeStruct((rows, width), jnp.bfloat16),
-        in_specs=[smem] + [vmem] * 9,
+        in_specs=[smem, smem] + [vmem] * 9,
         out_specs=vmem,
         scratch_shapes=[
             pltpu.VMEM((halves, (most + 2) * PATCH, LANES), jnp.float32),
             pltpu.VMEM((halves, most * PATCH, LANES), jnp.float32),
             pltpu.VMEM((most, width, PATCH), jnp.bfloat16),
-            pltpu.VMEM((most, PATCH, width), jnp.bfloat16),
+            pltpu.VMEM((most, 2, PATCH, width), jnp.bfloat16),
             pltpu.VMEM((halves, most * PATCH, LANES), jnp.float32),
             pltpu.VMEM((QTILE, width), jnp.float32),
+            pltpu.VMEM((most, 1, width), jnp.float32),
+            pltpu.VMEM((most, 1, width), jnp.float32),
         ],
         compiler_params=pltpu.CompilerParams(vmem_limit_bytes=56 << 20),
         name="attend",
-    )(scalars, moved, tail, head, gain_one, qkv, proj, gain_two, fc_one, fc_two)
-
-
-def passed_along(shard, by):
-    count = lax.axis_size(AXES)
-    pairs = [(i, i + by) for i in range(count) if 0 <= i + by < count]
-    return lax.ppermute(shard, AXES, pairs)
+    )(summary, count, moved, tail, head, gain_one, qkv, proj, gain_two, fc_one, fc_two)
 
 
 def per_device(
@@ -298,35 +463,20 @@
 ):
     rows, width = features.shape[2:]
     taps = neighbours.shape[2]
-    blocks = block_dest.shape[2]
-    devices = lax.axis_size(AXES)
-    me = lax.axis_index(AXES)
     own_count = counts.reshape(1)
-    place = block_dest.reshape(blocks)
-    target = place // blocks
-    label = jnp.stack([place % blocks, jnp.broadcast_to(own_count, (blocks,))], axis=1)
-    labels = jnp.zeros((devices, 2), jnp.int32).at[target].set(label)
-    labels = lax.all_to_all(labels, AXES, split_axis=0, concat_axis=0, tiled=True)
-    slots, every_count = labels[:, 0], labels[:, 1]
-    outgoing = convolved(
+    outgoing, notes = convolved(
         features.reshape(rows, width),
         neighbours.reshape(taps, rows),
-        target,
+        block_dest.reshape(-1),
+        own_count,
         conv_weight.reshape(taps * width, width),
         cpe_weight,
         cpe_gain.reshape(1, width),
     )
-    arrived = lax.all_to_all(outgoing, AXES, split_axis=0, concat_axis=0, tiled=True)
-    moved, tail = placed_rows(slots, own_count, arrived)
-    before = passed_along(tail, 1)
-    after = passed_along(moved[:PATCH], -1)
-    earlier = jnp.arange(devices) < me
-    offset = jnp.sum(jnp.where(earlier, every_count, 0))
-    known = jnp.sum(jnp.where(earlier, 0, every_count))
-    skew = offset % PATCH
-    scalars = jnp.stack([skew, own_count[0], known + skew])
+    moved, before, after, summary = exchanged(own_count, outgoing, notes)
     block_out = finished(
-        scalars,
+        summary,
+        own_count,
         moved,
         before,
         after,

time: 242 us -> 176 us (0.73)
  the two profiles are of different devices: /device:TPU:19 before, /device:TPU:56 now
where the time goes in v2:
time: 176 us
  Pallas kernels  169 us (96%)
  local copies, waits for them, and re-layouts  6.91 us (4%)
    pallas_call x1, Pallas kernels, finished(): pl.pallas_call(block_kernel, out_shape=jax.ShapeDtypeStruct((rows, width)...  95.1 us
    pallas_call x1, Pallas kernels, exchanged(): pl.pallas_call(exchange_kernel, out_shape=(jax.ShapeDtypeStruct((rows, wi...  44.5 us
    pallas_call x1, Pallas kernels, convolved(): pl.pallas_call(conv_kernel, out_shape=(jax.ShapeDtypeStruct((blocks, BLOC...  29 us
    unnamed x13, local copies, waits for them, and re-layouts  6.91 us

profile of v2, /device:TPU:56, one launch (start us, length us, event | category | flops | bytes accessed | tf_op | source)
XLA Modules:
  0.0 176.2 jit_solution(15291869068385076795)
XLA Ops:
  0.7 1.7 copy.16
  2.4 29.0 %convolve.1 = (bf16[128,16,256]{2,1,0:T(8,128)(2,1)}, s32[128,1,128]{2,1,0:T(1,128)}) custom-call(s32[128]{0:T(128)} %bitcast.20, s32[1]{0:T(128)} %bitcast.11.count_ref, s32[27,2048]{1,0:T(8,128)} %bitcast.15, bf16[2048,256]{1,0:T(8,128)(2,1)} %bitcast.16, bf16[6912,256]{1,0:T(8,128)(2,1)} %bitcast.14, bf16[256,256]{1,0:T(8,128)(2,1)} %cpe_ref.1, ...), custom_call_target="tpu_custom_call" | custom-call | tf_op jit(solution)/shard_map/convolve/pallas_call | solution.py:109
  31.4 0.0 copy-start.1
  31.4 1.2 copy-done.1
  32.6 0.0 copy-start.4
  32.6 0.8 copy-done.4
  33.4 44.5 %exchange.1 = (bf16[2048,256]{1,0:T(8,128)(2,1)S(1)}, bf16[1024,256]{1,0:T(8,128)(2,1)S(1)}, bf16[1024,256]{1,0:T(8,128)(2,1)S(1)}, s32[1,128]{1,0:T(1,128)S(1)}) custom-call(s32[1]{0:T(128)} %bitcast.12.count_ref, bf16[128,16,256]{2,1,0:T(8,128)(2,1)S(1)} %copy-done.1, s32[128,1,128]{2,1,0:T(1,128)S(1)} %copy-done.4), custom_call_target="tpu_custom_call" | custom-call | tf_op jit(solution)/shard_map/exchange/pallas_call | solution.py:240
  77.9 0.0 copy-start
  77.9 1.0 copy-done
  78.9 0.0 copy-start.2
  78.9 0.8 copy-done.2
  79.7 0.0 copy-start.3
  79.7 0.8 copy-done.3
  80.5 0.0 copy-start.5
  80.5 0.6 copy-done.5
  81.1 95.1 %attend.1 = bf16[2048,256]{1,0:T(8,128)(2,1)} custom-call(s32[1,128]{1,0:T(1,128)} %copy-done.5, s32[1]{0:T(128)} %bitcast.13.count_ref, bf16[2048,256]{1,0:T(8,128)(2,1)} %copy-done, bf16[1024,256]{1,0:T(8,128)(2,1)} %copy-done.2, bf16[1024,256]{1,0:T(8,128)(2,1)} %copy-done.3, f32[1,256]{1,0:T(1,128)} %bitcast.18, bf16[256,768]{1,0:T(8,128)(2,1)} %qkv_ref.1, ...), custom_call_target="tpu_custom_call" | custom-call | tf_op jit(solution)/shard_map/attend/pallas_call | solution.py:429
Async XLA Ops:
  31.4 1.2 copy-start.1
  32.6 0.8 copy-start.4
  77.9 1.0 copy-start
  78.9 0.8 copy-start.2
  79.7 0.8 copy-start.3
  80.5 0.6 copy-start.5

commit v3 on v2

--- a/solution.py
+++ b/solution.py
@@ -1,3 +1,5 @@
+import functools
+
 import jax
 import jax.numpy as jnp
 from jax import lax
@@ -8,11 +10,12 @@
 HEADS = 16
 PATCH = 1024
 BLOCK = 16
-SUPER = 512
+SUPER = 1024
 TILE = 128
 WINDOW = 256
 QTILE = 256
 LANES = 128
+STACK = 2
 SAFE_SCORE = 30.0
 SAFE_VALUE = 1e20
 
@@ -43,52 +46,79 @@
     out_ref,
     notes_ref,
     picked_ref,
+    columns_ref,
+    lows_ref,
+    passes_ref,
+    held_ref,
+    held_sem,
 ):
     taps, span = taps_ref.shape
     total, width = rows_ref.shape
     blocks = out_ref.shape[0]
     step = pl.program_id(0)
+    fetch = pltpu.make_async_copy(weight_ref, held_ref, held_sem)
+
+    @pl.when(step == 0)
+    def _():
+        fetch.start()
+
     note_lane = lax.broadcasted_iota(jnp.int32, (1, LANES), 1)
     lanes = lax.broadcasted_iota(jnp.int32, (TILE, WINDOW), 1)
 
-    for part in range(span // TILE):
+    def columns_of(part):
         chunk = taps_ref[:, part * TILE : (part + 1) * TILE]
+        spare = jnp.full((-taps % 8, TILE), total, jnp.int32)
+        return chunk, jnp.concatenate([chunk, spare], axis=0).T
+
+    def reach(chunk):
         as_float = chunk.astype(jnp.float32)
-        low = jnp.min(as_float).astype(jnp.int32)
+        low = jnp.min(as_float).astype(jnp.int32) // BLOCK * BLOCK
         high = jnp.max(jnp.where(chunk < total, as_float, -1.0)).astype(jnp.int32)
-        low = low // BLOCK * BLOCK
         passes = (high - low + WINDOW) // WINDOW
-        low = jnp.minimum(low, total - passes * WINDOW)
-        filled = jnp.concatenate(
-            [chunk, jnp.full((-taps % 8, TILE), total, jnp.int32)], axis=0
-        )
-        columns = filled.T
-        here = pl.ds(part * TILE, TILE)
-
-        def pick(start):
-            window = rows_ref[pl.ds(pl.multiple_of(start, BLOCK), WINDOW), :]
-            shifted = columns - start
-            hot = jnp.concatenate(
-                [
-                    jnp.where(shifted[:, tap : tap + 1] == lanes, 1.0, 0.0).astype(jnp.bfloat16)
-                    for tap in range(taps)
-                ],
-                axis=0,
-            )
-            return jnp.dot(hot, window, preferred_element_type=jnp.float32).astype(jnp.bfloat16)
-
-        first = pick(low)
+        return jnp.minimum(low, total - passes * WINDOW), passes
+
+    def pick(columns, start):
+        window = rows_ref[pl.ds(pl.multiple_of(start, BLOCK), WINDOW), :]
+        shifted = columns - start
+        return [
+            jnp.dot(
+                jnp.where(shifted[:, tap : tap + 1] == lanes, 1.0, 0.0).astype(jnp.bfloat16),
+                window,
+                preferred_element_type=jnp.float32,
+            ).astype(jnp.bfloat16)
+            for tap in range(taps)
+        ]
+
+    parts = [columns_of(part) for part in range(span // TILE)]
+    ranges = [reach(chunk) for chunk, _ in parts]
+    for part, (low, passes) in enumerate(ranges):
+        first = pick(parts[part][1], low)
         for tap in range(taps):
-            picked_ref[here, tap * width : (tap + 1) * width] = first[tap * TILE : (tap + 1) * TILE]
-
-        @pl.loop(1, passes)
-        def _(index):
-            more = pick(low + index * WINDOW)
-            for tap in range(taps):
-                columns_here = slice(tap * width, (tap + 1) * width)
-                picked_ref[here, columns_here] += more[tap * TILE : (tap + 1) * TILE]
-
-    summed = jnp.dot(picked_ref[...], weight_ref[...], preferred_element_type=jnp.float32)
+            picked_ref[part * TILE : (part + 1) * TILE, tap * width : (tap + 1) * width] = first[tap]
+        lows_ref[part] = low
+        passes_ref[part] = passes
+
+    @pl.when(functools.reduce(jnp.maximum, [passes for _, passes in ranges]) > 1)
+    def _():
+        for part in range(span // TILE):
+            columns_ref[part] = parts[part][1]
+
+        @pl.loop(0, span // TILE)
+        def _(part):
+            here = pl.ds(pl.multiple_of(part * TILE, TILE), TILE)
+
+            @pl.loop(1, passes_ref[part])
+            def _(index):
+                more = pick(columns_ref[part], lows_ref[part] + index * WINDOW)
+                for tap in range(taps):
+                    columns = slice(tap * width, (tap + 1) * width)
+                    picked_ref[here, columns] += more[tap]
+
+    @pl.when(step == 0)
+    def _():
+        fetch.wait()
+
+    summed = jnp.dot(picked_ref[...], held_ref[...], preferred_element_type=jnp.float32)
     linear = jnp.dot(
         summed.astype(jnp.bfloat16), cpe_ref[...], preferred_element_type=jnp.float32
     )
@@ -118,7 +148,7 @@
             in_specs=[
                 pl.BlockSpec((taps, SUPER), lambda step, *_: (0, step)),
                 pl.BlockSpec((total, width), whole),
-                pl.BlockSpec((taps * width, width), whole),
+                pl.BlockSpec(memory_space=pltpu.HBM),
                 pl.BlockSpec((width, width), whole),
                 pl.BlockSpec((1, width), whole),
             ],
@@ -126,9 +156,16 @@
                 pl.BlockSpec((blocks, BLOCK, width), lambda step, *_: (0, 0, 0)),
                 pl.BlockSpec((blocks, 1, LANES), lambda step, *_: (0, 0, 0)),
             ),
-            scratch_shapes=[pltpu.VMEM((SUPER, taps * width), jnp.bfloat16)],
+            scratch_shapes=[
+                pltpu.VMEM((SUPER, taps * width), jnp.bfloat16),
+                pltpu.VMEM((SUPER // TILE, TILE, taps + -taps % 8), jnp.int32),
+                pltpu.SMEM((SUPER // TILE,), jnp.int32),
+                pltpu.SMEM((SUPER // TILE,), jnp.int32),
+                pltpu.VMEM((taps * width, width), jnp.bfloat16),
+                pltpu.SemaphoreType.DMA,
+            ],
         ),
-        compiler_params=pltpu.CompilerParams(vmem_limit_bytes=56 << 20),
+        compiler_params=pltpu.CompilerParams(vmem_limit_bytes=40 << 20),
         name="convolve",
     )(dest, count, neighbours, features, conv_weight, cpe_weight, cpe_gain)
 
@@ -174,6 +211,18 @@
 
     block_sems = (send_sem, recv_sem)
     note_sems = (note_send_sem, note_recv_sem)
+
+    barrier = pltpu.get_barrier_semaphore()
+
+    def greet(step, _):
+        peer = place_of((me + step) % devices)
+        pl.semaphore_signal(
+            barrier, inc=1, device_id=peer, device_id_type=pl.DeviceIdType.MESH
+        )
+        return 0
+
+    lax.fori_loop(1, devices, greet, 0)
+    pl.semaphore_wait(barrier, devices - 1)
 
     def send(step, _):
         peer = (me + step) % devices
@@ -263,7 +312,7 @@
             dma,
         ],
         compiler_params=pltpu.CompilerParams(
-            vmem_limit_bytes=32 << 20, has_side_effects=True
+            vmem_limit_bytes=32 << 20, has_side_effects=True, collective_id=0
         ),
         name="exchange",
     )(count, outgoing, notes)
@@ -347,65 +396,13 @@
             size_ref[patch] = size if part == 0 else jnp.maximum(size_ref[patch], size)
 
 
-    @pl.loop(skew // QTILE, (skew + rows + QTILE - 1) // QTILE)
-    def _(tile):
-        start = pl.multiple_of(tile * QTILE, QTILE)
-        here = get(own_ref, start, QTILE)
-        gathered_ref[...] = jnp.zeros((QTILE, width), jnp.float32)
-
-        @pl.when(start < live_end)
-        def _():
-            patch = tile // per_patch
-            normed = normalised(here, gain_one_ref[...]).astype(jnp.bfloat16)
-            queries = jnp.dot(normed, qkv_ref[:, :width], preferred_element_type=jnp.float32)
-            queries = queries.astype(jnp.bfloat16) * jnp.bfloat16((width // HEADS) ** -0.5)
-            reach = jnp.max(squares(queries) * reach_ref[patch])
-            safe = (reach <= SAFE_SCORE**2) & (jnp.max(size_ref[patch]) <= SAFE_VALUE)
-
-            def gather(group, odd, softened):
-                heads = [2 * (group * 2 + index) + odd for index in range(2)]
-                one = jnp.concatenate(
-                    [jnp.where(head_of_lane == head, queries, jnp.bfloat16(0)) for head in heads],
-                    axis=0,
-                )
-                scores = jnp.dot(one, keys_ref[patch], preferred_element_type=jnp.float32)
-                grown = softened(scores).astype(jnp.bfloat16)
-                mixed = jnp.dot(grown, values_ref[patch, odd], preferred_element_type=jnp.float32)
-                spare = LANES - 1 if odd == 0 else 0
-                mixed = mixed * (1.0 / mixed[:, spare : spare + 1])
-                so_far = gathered_ref[...]
-                for index, head in enumerate(heads):
-                    piece = mixed[index * QTILE : (index + 1) * QTILE]
-                    so_far = jnp.where(head_of_lane == head, piece, so_far)
-                gathered_ref[...] = so_far
-
-            @pl.when(safe)
-            def _():
-                @pl.loop(0, HEADS // 4, unroll=4)
-                def _(group):
-                    for odd in range(2):
-                        gather(group, odd, jnp.exp)
-
-            @pl.when(jnp.logical_not(safe))
-            def _():
-                spot = patch * PATCH + lax.broadcasted_iota(jnp.int32, (1, PATCH), 1)
-                bias = jnp.where(spot < known, 0.0, -1e30)
-
-                def softened(scores):
-                    scores = scores + bias
-                    return jnp.exp(scores - jnp.max(scores, axis=-1, keepdims=True))
-
-                @pl.loop(0, HEADS // 4)
-                def _(group):
-                    for odd in range(2):
-                        gather(group, odd, softened)
-
+    def finish(start):
         spots = start + lax.broadcasted_iota(jnp.int32, (QTILE, 1), 0)
         attended = jnp.where(spots < live_end, gathered_ref[...], 0.0)
         projected = jnp.dot(
             attended.astype(jnp.bfloat16), proj_ref[...], preferred_element_type=jnp.float32
         )
-        mixed = (here + projected).astype(jnp.bfloat16).astype(jnp.float32)
+        mixed = (get(own_ref, start, QTILE) + projected).astype(jnp.bfloat16).astype(jnp.float32)
         normed = normalised(mixed, gain_two_ref[...]).astype(jnp.bfloat16)
         hidden = jnp.dot(normed, fc_one_ref[...], preferred_element_type=jnp.float32)
         hidden = 0.5 * hidden * (1.0 + lax.erf(hidden * 0.5**0.5))
@@ -413,6 +410,66 @@
             hidden.astype(jnp.bfloat16), fc_two_ref[...], preferred_element_type=jnp.float32
         )
         put(result_ref, start, final)
+
+    first_tile = skew // QTILE
+    live_tiles = (live_end + QTILE - 1) // QTILE
+    all_tiles = (skew + rows + QTILE - 1) // QTILE
+
+    @pl.loop(first_tile, live_tiles)
+    def _(tile):
+        start = pl.multiple_of(tile * QTILE, QTILE)
+        before = pl.multiple_of(jnp.maximum(tile - 1, 0) * QTILE, QTILE)
+        patch = tile // per_patch
+        normed = normalised(get(own_ref, start, QTILE), gain_one_ref[...]).astype(jnp.bfloat16)
+        queries = jnp.dot(normed, qkv_ref[:, :width], preferred_element_type=jnp.float32)
+        queries = queries.astype(jnp.bfloat16) * jnp.bfloat16((width // HEADS) ** -0.5)
+        reach = jnp.max(squares(queries) * reach_ref[patch])
+        safe = (reach <= SAFE_SCORE**2) & (jnp.max(size_ref[patch]) <= SAFE_VALUE)
+
+        def gather(group, odd, softened, so_far):
+            heads = [2 * (group * STACK + index) + odd for index in range(STACK)]
+            one = jnp.concatenate(
+                [jnp.where(head_of_lane == head, queries, jnp.bfloat16(0)) for head in heads],
+                axis=0,
+            )
+            scores = jnp.dot(one, keys_ref[patch], preferred_element_type=jnp.float32)
+            grown = softened(scores).astype(jnp.bfloat16)
+            mixed = jnp.dot(grown, values_ref[patch, odd], preferred_element_type=jnp.float32)
+            spare = LANES - 1 if odd == 0 else 0
+            mixed = mixed * (1.0 / mixed[:, spare : spare + 1])
+            for index, head in enumerate(heads):
+                piece = mixed[index * QTILE : (index + 1) * QTILE]
+                so_far = jnp.where(head_of_lane == head, piece, so_far)
+            return so_far
+
+        @pl.when(safe)
+        def _():
+            finish(before)
+            so_far = jnp.zeros((QTILE, width), jnp.float32)
+            for group in range(HEADS // (2 * STACK)):
+                for odd in range(2):
+                    so_far = gather(group, odd, jnp.exp, so_far)
+            gathered_ref[...] = so_far
+
+        @pl.when(jnp.logical_not(safe))
+        def _():
+            finish(before)
+            spot = patch * PATCH + lax.broadcasted_iota(jnp.int32, (1, PATCH), 1)
+            bias = jnp.where(spot < known, 0.0, -1e30)
+
+            def softened(scores):
+                scores = scores + bias
+                return jnp.exp(scores - jnp.max(scores, axis=-1, keepdims=True))
+
+            @pl.loop(0, HEADS // (2 * STACK))
+            def _(group):
+                for odd in range(2):
+                    gathered_ref[...] = gather(group, odd, softened, gathered_ref[...])
+
+    @pl.loop(live_tiles - 1, all_tiles)
+    def _(tile):
+        finish(pl.multiple_of(tile * QTILE, QTILE))
+        gathered_ref[...] = jnp.zeros((QTILE, width), jnp.float32)
 
     for part in range(rows // QTILE):
         out_ref[part * QTILE : (part + 1) * QTILE, :] = get(
@@ -441,7 +498,7 @@
             pltpu.VMEM((most, 1, width), jnp.float32),
             pltpu.VMEM((most, 1, width), jnp.float32),
         ],
-        compiler_params=pltpu.CompilerParams(vmem_limit_bytes=56 << 20),
+        compiler_params=pltpu.CompilerParams(vmem_limit_bytes=36 << 20),
         name="attend",
     )(summary, count, moved, tail, head, gain_one, qkv, proj, gain_two, fc_one, fc_two)
 

time: 176 us -> 165 us (0.938)
  the two profiles are of different devices: /device:TPU:56 before, /device:TPU:24 now
where the time goes in v3:
time: 165 us
  Pallas kernels  158 us (96%)
  local copies, waits for them, and re-layouts  6.49 us (4%)
    pallas_call x1, Pallas kernels, finished(): pl.pallas_call(block_kernel, out_shape=jax.ShapeDtypeStruct((rows, width)...  94.3 us
    pallas_call x1, Pallas kernels, exchanged(): pl.pallas_call(exchange_kernel, out_shape=(jax.ShapeDtypeStruct((rows, wi...  43.6 us
    pallas_call x1, Pallas kernels, convolved(): pl.pallas_call(conv_kernel, out_shape=(jax.ShapeDtypeStruct((blocks, BLOC...  19.7 us
    unnamed x23, local copies, waits for them, and re-layouts  6.49 us

profile of v3, /device:TPU:24, one launch (start us, length us, event | category | flops | bytes accessed | tf_op | source)
XLA Modules:
  0.0 164.9 jit_solution(9559229536530228457)
XLA Ops:
  0.0 0.0 copy-start.9
  0.0 0.0 copy-start.4
  0.0 0.0 copy-start.8
  0.7 1.0 copy.16
  1.7 0.0 copy-start
  1.7 2.0 %copy-done = bf16[27,256,256]{2,1,0:T(8,128)(2,1)S(1)} copy-done((bf16[27,256,256]{2,1,0:T(8,128)(2,1)S(1)}, bf16[27,256,256]{2,1,0:T(8,128)(2,1)}, u32[]{:S(2)}) %copy-start) | copy-done | bytes 3538968
  3.7 0.0 copy-start.1
  3.7 1.2 copy-done.1
  5.0 0.0 copy-start.5
  5.0 0.9 copy-done.5
  5.9 0.0 copy-start.7
  5.9 0.7 copy-done.7
  6.5 0.0 copy-start.10
  6.5 0.7 copy-done.10
  7.2 0.0 copy-start.2
  7.2 0.0 copy-start.3
  7.2 0.0 copy-start.6
  7.2 19.7 %convolve.1 = (bf16[128,16,256]{2,1,0:T(8,128)(2,1)S(1)}, s32[128,1,128]{2,1,0:T(1,128)S(1)}) custom-call(s32[128]{0:T(128)S(1)} %bitcast.20, s32[1]{0:T(128)} %bitcast.11.count_ref, s32[27,2048]{1,0:T(8,128)S(1)} %bitcast.15, bf16[2048,256]{1,0:T(8,128)(2,1)S(1)} %bitcast.16, bf16[6912,256]{1,0:T(8,128)(2,1)S(1)} %bitcast.14, ...), custom_call_target="tpu_custom_call" | custom-call | tf_op jit(solution)/shard_map/convolve/pallas_call | solution.py:139
  26.9 43.6 %exchange.1 = (bf16[2048,256]{1,0:T(8,128)(2,1)S(1)}, bf16[1024,256]{1,0:T(8,128)(2,1)S(1)}, bf16[1024,256]{1,0:T(8,128)(2,1)S(1)}, s32[1,128]{1,0:T(1,128)S(1)}) custom-call(s32[1]{0:T(128)} %bitcast.12.count_ref, bf16[128,16,256]{2,1,0:T(8,128)(2,1)S(1)} %get-tuple-element.11.outgoing_ref, s32[128,1,128]{2,1,0:T(1,128)S(1)} %get-tuple-element.12.notes_ref), custom_call_target="tpu_custom_call" | custom-call | tf_op jit(solution)/shard_map/exchange/pallas_call | solution.py:289
  70.5 0.0 copy-done.9
  70.5 0.0 copy-done.4
  70.5 0.0 copy-done.8
  70.6 0.0 copy-done.2
  70.6 0.0 copy-done.3
  70.6 0.0 copy-done.6
  70.6 94.3 %attend.1 = bf16[2048,256]{1,0:T(8,128)(2,1)} custom-call(s32[1,128]{1,0:T(1,128)S(1)} %get-tuple-element.13.summary_ref, s32[1]{0:T(128)} %bitcast.13.count_ref, bf16[2048,256]{1,0:T(8,128)(2,1)S(1)} %get-tuple-element.14.moved_ref, bf16[1024,256]{1,0:T(8,128)(2,1)S(1)} %get-tuple-element.15.tail_ref, bf16[1024,256]{1,0:T(8,128)(2,1)S(1)} %get-tuple-element.16.head_ref, ...), custom_call_target="tpu_custom_call" | custom-call | tf_op jit(solution)/shard_map/attend/pallas_call | solution.py:486
Async XLA Ops:
  0.0 70.5 %copy-start.9 = (f32[256]{0:T(256)S(1)}, f32[256]{0:T(256)}, u32[]{:S(2)}) copy-start(f32[256]{0:T(256)} %param.23) | copy-start | bytes 3076
  0.0 70.5 %copy-start.4 = (bf16[256,768]{1,0:T(8,128)(2,1)S(1)}, bf16[256,768]{1,0:T(8,128)(2,1)}, u32[]{:S(2)}) copy-start(bf16[256,768]{1,0:T(8,128)(2,1)} %qkv_ref.1) | copy-start | bytes 1179652
  0.0 70.5 %copy-start.8 = (f32[256]{0:T(256)S(1)}, f32[256]{0:T(256)}, u32[]{:S(2)}) copy-start(f32[256]{0:T(256)} %param.20) | copy-start | bytes 3076
  1.7 2.0 %copy-start = (bf16[27,256,256]{2,1,0:T(8,128)(2,1)S(1)}, bf16[27,256,256]{2,1,0:T(8,128)(2,1)}, u32[]{:S(2)}) copy-start(bf16[27,256,256]{2,1,0:T(8,128)(2,1)} %param.17) | copy-start | bytes 10616836
  3.7 1.2 copy-start.1
  5.0 0.9 copy-start.5
  5.9 0.7 copy-start.7
  6.5 0.7 copy-start.10
  7.2 63.4 %copy-start.2 = (bf16[256,1024]{1,0:T(8,128)(2,1)S(1)}, bf16[256,1024]{1,0:T(8,128)(2,1)}, u32[]{:S(2)}) copy-start(bf16[256,1024]{1,0:T(8,128)(2,1)} %fc_one_ref.1) | copy-start | bytes 1572868
  7.2 63.4 %copy-start.3 = (bf16[1024,256]{1,0:T(8,128)(2,1)S(1)}, bf16[1024,256]{1,0:T(8,128)(2,1)}, u32[]{:S(2)}) copy-start(bf16[1024,256]{1,0:T(8,128)(2,1)} %fc_two_ref.1) | copy-start | bytes 1572868
  7.2 63.4 %copy-start.6 = (bf16[256,256]{1,0:T(8,128)(2,1)S(1)}, bf16[256,256]{1,0:T(8,128)(2,1)}, u32[]{:S(2)}) copy-start(bf16[256,256]{1,0:T(8,128)(2,1)} %proj_ref.1) | copy-start | bytes 393220

commit v4 on v3

--- a/solution.py
+++ b/solution.py
@@ -41,9 +41,8 @@
     taps_ref,
     rows_ref,
     weight_ref,
-    cpe_ref,
-    gain_ref,
     out_ref,
+    own_ref,
     notes_ref,
     picked_ref,
     columns_ref,
@@ -52,7 +51,8 @@
     held_ref,
     held_sem,
 ):
-    taps, span = taps_ref.shape
+    taps, tiles, _ = taps_ref.shape
+    span = tiles * TILE
     total, width = rows_ref.shape
     blocks = out_ref.shape[0]
     step = pl.program_id(0)
@@ -66,7 +66,7 @@
     lanes = lax.broadcasted_iota(jnp.int32, (TILE, WINDOW), 1)
 
     def columns_of(part):
-        chunk = taps_ref[:, part * TILE : (part + 1) * TILE]
+        chunk = taps_ref[:, part, :]
         spare = jnp.full((-taps % 8, TILE), total, jnp.int32)
         return chunk, jnp.concatenate([chunk, spare], axis=0).T
 
@@ -119,40 +119,39 @@
         fetch.wait()
 
     summed = jnp.dot(picked_ref[...], held_ref[...], preferred_element_type=jnp.float32)
-    linear = jnp.dot(
-        summed.astype(jnp.bfloat16), cpe_ref[...], preferred_element_type=jnp.float32
-    )
-    own = rows_ref[pl.ds(pl.multiple_of(step * span, span), span), :].astype(jnp.float32)
-    encoded = (own + normalised(linear, gain_ref[...])).astype(jnp.bfloat16)
+    summed = summed.astype(jnp.bfloat16)
+    own = rows_ref[pl.ds(pl.multiple_of(step * span, span), span), :]
     for block in range(span // BLOCK):
         place = dest_ref[step * (span // BLOCK) + block]
         target, slot = place // blocks, place % blocks
-        out_ref[target] = encoded[block * BLOCK : (block + 1) * BLOCK]
+        out_ref[target] = summed[block * BLOCK : (block + 1) * BLOCK]
+        own_ref[target] = own[block * BLOCK : (block + 1) * BLOCK]
         notes_ref[target] = jnp.where(note_lane == 0, slot, count_ref[0])
 
 
-def convolved(features, neighbours, dest, count, conv_weight, cpe_weight, cpe_gain):
+def convolved(features, neighbours, dest, count, conv_weight):
     total, width = features.shape
     taps = neighbours.shape[0]
+    shape = jax.ShapeDtypeStruct((total // BLOCK, BLOCK, width), jnp.bfloat16)
     blocks = total // BLOCK
     whole = lambda step, *_: (0, 0)
     return pl.pallas_call(
         conv_kernel,
         out_shape=(
-            jax.ShapeDtypeStruct((blocks, BLOCK, width), jnp.bfloat16),
+            shape,
+            shape,
             jax.ShapeDtypeStruct((blocks, 1, LANES), jnp.int32),
         ),
         grid_spec=pltpu.PrefetchScalarGridSpec(
             num_scalar_prefetch=2,
             grid=(total // SUPER,),
             in_specs=[
-                pl.BlockSpec((taps, SUPER), lambda step, *_: (0, step)),
+                pl.BlockSpec((taps, SUPER // TILE, TILE), lambda step, *_: (0, step, 0)),
                 pl.BlockSpec((total, width), whole),
                 pl.BlockSpec(memory_space=pltpu.HBM),
-                pl.BlockSpec((width, width), whole),
-                pl.BlockSpec((1, width), whole),
             ],
             out_specs=(
+                pl.BlockSpec((blocks, BLOCK, width), lambda step, *_: (0, 0, 0)),
                 pl.BlockSpec((blocks, BLOCK, width), lambda step, *_: (0, 0, 0)),
                 pl.BlockSpec((blocks, 1, LANES), lambda step, *_: (0, 0, 0)),
             ),
@@ -167,17 +166,23 @@
         ),
         compiler_params=pltpu.CompilerParams(vmem_limit_bytes=40 << 20),
         name="convolve",
-    )(dest, count, neighbours, features, conv_weight, cpe_weight, cpe_gain)
+    )(dest, count, neighbours, features, conv_weight)
 
 
 def exchange_kernel(
     count_ref,
-    outgoing_ref,
+    summed_ref,
+    own_ref,
     notes_ref,
+    cpe_ref,
+    cpe_gain_ref,
+    gain_ref,
     moved_ref,
+    normed_ref,
     before_ref,
     after_ref,
     summary_ref,
+    outgoing_ref,
     arrived_ref,
     heard_ref,
     wide_ref,
@@ -222,6 +227,18 @@
         return 0
 
     lax.fori_loop(1, devices, greet, 0)
+
+    def encode(part, _):
+        here = pl.ds(part * (QTILE // BLOCK), QTILE // BLOCK)
+        linear = jnp.dot(
+            summed_ref[here].reshape(QTILE, -1), cpe_ref[...], preferred_element_type=jnp.float32
+        )
+        own = own_ref[here].reshape(QTILE, -1).astype(jnp.float32)
+        encoded = (own + normalised(linear, cpe_gain_ref[...])).astype(jnp.bfloat16)
+        outgoing_ref[here] = encoded.reshape(QTILE // BLOCK, BLOCK, -1)
+        return 0
+
+    lax.fori_loop(0, devices * BLOCK // QTILE, encode, 0)
     pl.semaphore_wait(barrier, devices - 1)
 
     def send(step, _):
@@ -257,7 +274,6 @@
         block = arrived_ref[order_ref[0, slot]]
         row = pl.multiple_of(slot * BLOCK, BLOCK)
         moved_ref[pl.ds(row, BLOCK), :] = block
-        put(wide_ref, row, block.astype(jnp.float32))
         return 0
 
     lax.fori_loop(0, devices, settle, 0)
@@ -265,8 +281,15 @@
     previous = (me + devices - 1) % devices
     head_sems = (side_send_sem.at[0], side_recv_sem.at[0])
     tail_sems = (side_send_sem.at[1], side_recv_sem.at[1])
-    head = to_peer(moved_ref.at[pl.ds(0, PATCH)], after_ref, head_sems, previous)
-    head.start()
+    head = to_peer(normed_ref.at[pl.ds(0, PATCH)], after_ref, head_sems, previous)
+    for part in range(moved_ref.shape[0] // QTILE):
+        here = slice(part * QTILE, (part + 1) * QTILE)
+        normed = normalised(moved_ref[here, :].astype(jnp.float32), gain_ref[...])
+        normed = normed.astype(jnp.bfloat16)
+        normed_ref[here, :] = normed
+        put(wide_ref, part * QTILE, normed.astype(jnp.float32))
+        if (part + 1) * QTILE == PATCH:
+            head.start()
     start = jnp.clip(count_ref[0] - PATCH, 0, moved_ref.shape[0] - PATCH)
     for part in range(PATCH // QTILE):
         piece = get(wide_ref, start + part * QTILE, QTILE)
@@ -279,24 +302,27 @@
     tail.wait()
 
 
-def exchanged(count, outgoing, notes):
-    blocks, block, width = outgoing.shape
+def exchanged(count, summed, own, notes, cpe_weight, cpe_gain, gain):
+    blocks, block, width = summed.shape
     rows = blocks * block
     vmem = pl.BlockSpec(memory_space=pltpu.VMEM)
     smem = pl.BlockSpec(memory_space=pltpu.SMEM)
+    whole = jax.ShapeDtypeStruct((rows, width), jnp.bfloat16)
     side = jax.ShapeDtypeStruct((PATCH, width), jnp.bfloat16)
     dma = pltpu.SemaphoreType.DMA
     return pl.pallas_call(
         exchange_kernel,
         out_shape=(
-            jax.ShapeDtypeStruct((rows, width), jnp.bfloat16),
+            whole,
+            whole,
             side,
             side,
             jax.ShapeDtypeStruct((1, LANES), jnp.int32),
         ),
-        in_specs=[smem, vmem, vmem],
-        out_specs=(vmem, vmem, vmem, vmem),
+        in_specs=[smem] + [vmem] * 6,
+        out_specs=(vmem,) * 5,
         scratch_shapes=[
+            pltpu.VMEM((blocks, block, width), jnp.bfloat16),
             pltpu.VMEM((blocks, block, width), jnp.bfloat16),
             pltpu.VMEM((blocks, 1, LANES), jnp.int32),
             pltpu.VMEM((width // LANES, rows, LANES), jnp.float32),
@@ -315,16 +341,16 @@
             vmem_limit_bytes=32 << 20, has_side_effects=True, collective_id=0
         ),
         name="exchange",
-    )(count, outgoing, notes)
+    )(count, summed, own, notes, cpe_weight, cpe_gain, gain)
 
 
 def block_kernel(
     summary_ref,
     count_ref,
     moved_ref,
+    normed_ref,
     tail_ref,
     head_ref,
-    gain_one_ref,
     qkv_ref,
     proj_ref,
     gain_two_ref,
@@ -351,8 +377,9 @@
         put(source_ref, skew + part * QTILE, piece)
     for part in range(rows // QTILE):
         piece = moved_ref[part * QTILE : (part + 1) * QTILE, :].astype(jnp.float32)
+        put(own_ref, skew + part * QTILE, piece)
+        piece = normed_ref[part * QTILE : (part + 1) * QTILE, :].astype(jnp.float32)
         put(source_ref, PATCH + skew + part * QTILE, piece)
-        put(own_ref, skew + part * QTILE, piece)
     for part in range(PATCH // QTILE):
         piece = head_ref[part * QTILE : (part + 1) * QTILE, :].astype(jnp.float32)
         put(source_ref, PATCH + live_end + part * QTILE, piece)
@@ -376,9 +403,8 @@
     def _(patch):
         for part in range(per_patch):
             start = pl.multiple_of(PATCH + patch * PATCH + part * QTILE, QTILE)
-            normed = normalised(get(source_ref, start, QTILE), gain_one_ref[...])
             pair = jnp.dot(
-                normed.astype(jnp.bfloat16),
+                get(source_ref, start, QTILE).astype(jnp.bfloat16),
                 qkv_ref[:, width:],
                 preferred_element_type=jnp.float32,
             )
@@ -420,7 +446,7 @@
         start = pl.multiple_of(tile * QTILE, QTILE)
         before = pl.multiple_of(jnp.maximum(tile - 1, 0) * QTILE, QTILE)
         patch = tile // per_patch
-        normed = normalised(get(own_ref, start, QTILE), gain_one_ref[...]).astype(jnp.bfloat16)
+        normed = get(source_ref, pl.multiple_of(PATCH + start, QTILE), QTILE).astype(jnp.bfloat16)
         queries = jnp.dot(normed, qkv_ref[:, :width], preferred_element_type=jnp.float32)
         queries = queries.astype(jnp.bfloat16) * jnp.bfloat16((width // HEADS) ** -0.5)
         reach = jnp.max(squares(queries) * reach_ref[patch])
@@ -477,7 +503,7 @@
         ).astype(jnp.bfloat16)
 
 
-def finished(summary, count, moved, tail, head, gain_one, qkv, proj, gain_two, fc_one, fc_two):
+def finished(summary, count, moved, normed, tail, head, qkv, proj, gain_two, fc_one, fc_two):
     rows, width = moved.shape
     vmem = pl.BlockSpec(memory_space=pltpu.VMEM)
     smem = pl.BlockSpec(memory_space=pltpu.SMEM)
@@ -500,7 +526,7 @@
         ],
         compiler_params=pltpu.CompilerParams(vmem_limit_bytes=36 << 20),
         name="attend",
-    )(summary, count, moved, tail, head, gain_one, qkv, proj, gain_two, fc_one, fc_two)
+    )(summary, count, moved, normed, tail, head, qkv, proj, gain_two, fc_one, fc_two)
 
 
 def per_device(
@@ -520,24 +546,33 @@
 ):
     rows, width = features.shape[2:]
     taps = neighbours.shape[2]
+    def afar(value):
+        return pltpu.with_memory_space_constraint(value, pltpu.HBM)
+
     own_count = counts.reshape(1)
-    outgoing, notes = convolved(
-        features.reshape(rows, width),
-        neighbours.reshape(taps, rows),
-        block_dest.reshape(-1),
+    summed, own, notes = convolved(
+        afar(features.reshape(rows, width)),
+        afar(neighbours.reshape(taps, rows // TILE, TILE)),
+        afar(block_dest.reshape(-1)),
         own_count,
-        conv_weight.reshape(taps * width, width),
+        afar(conv_weight.reshape(taps * width, width)),
+    )
+    moved, normed, before, after, summary = exchanged(
+        own_count,
+        summed,
+        own,
+        notes,
         cpe_weight,
         cpe_gain.reshape(1, width),
+        norm1_gain.reshape(1, width),
     )
-    moved, before, after, summary = exchanged(own_count, outgoing, notes)
     block_out = finished(
         summary,
         own_count,
         moved,
+        normed,
         before,
         after,
-        norm1_gain.reshape(1, width),
         qkv_weight,
         proj_weight,
         norm2_gain.reshape(1, width),

time: 165 us -> 156 us (0.945)
  the two profiles are of different devices: /device:TPU:24 before, /device:TPU:27 now
where the time goes in v4:
time: 156 us
  Pallas kernels  155 us (99%)
    pallas_call x1, Pallas kernels, finished(): pl.pallas_call(block_kernel, out_shape=jax.ShapeDtypeStruct((rows, width)...  91.7 us
    pallas_call x1, Pallas kernels, exchanged(): pl.pallas_call(exchange_kernel, out_shape=(whole, whole, side, side, jax....  43 us
    pallas_call x1, Pallas kernels, convolved(): pl.pallas_call(conv_kernel, out_shape=(shape, shape, jax.ShapeDtypeStruct...  20.1 us

profile of v4, /device:TPU:27, one launch (start us, length us, event | category | flops | bytes accessed | tf_op | source)
XLA Modules:
  0.0 155.7 jit_solution(6757014380110784591)
XLA Ops:
  0.0 0.0 copy-start.6
  0.0 0.0 copy-start.5
  0.0 0.0 copy-start.3
  0.7 0.0 copy-start
  0.7 0.0 copy-start.1
  0.7 0.0 copy-start.2
  0.7 0.0 copy-start.4
  0.7 0.0 copy-start.7
  0.7 20.1 %convolve.1 = (bf16[128,16,256]{2,1,0:T(8,128)(2,1)S(1)}, bf16[128,16,256]{2,1,0:T(8,128)(2,1)S(1)}, s32[128,1,128]{2,1,0:T(1,128)S(1)}) custom-call(s32[128]{0:T(128)} %bitcast.18, s32[1]{0:T(128)} %bitcast.9.count_ref, s32[27,16,128]{2,1,0:T(8,128)} %bitcast.17, bf16[2048,256]{1,0:T(8,128)(2,1)} %bitcast.16, bf16[6912,256]{1,0:T(8,128)(2,1)} %bitcast.15), custom_call_target="tpu_custom_call" | custom-call | tf_op jit(solution)/shard_map/convolve/pallas_call | solution.py:138
  20.9 0.0 copy-done.6
  20.9 0.0 copy-done.5
  20.9 0.0 copy-done.3
  20.9 43.0 %exchange.1 = (bf16[2048,256]{1,0:T(8,128)(2,1)S(1)}, bf16[2048,256]{1,0:T(8,128)(2,1)S(1)}, bf16[1024,256]{1,0:T(8,128)(2,1)S(1)}, bf16[1024,256]{1,0:T(8,128)(2,1)S(1)}, s32[1,128]{1,0:T(1,128)S(1)}) custom-call(s32[1]{0:T(128)} %bitcast.10.count_ref, bf16[128,16,256]{2,1,0:T(8,128)(2,1)S(1)} %get-tuple-element.13.summed_ref, ...), custom_call_target="tpu_custom_call" | custom-call | tf_op jit(solution)/shard_map/exchange/pallas_call | solution.py:313
  63.9 0.0 copy-done
  63.9 0.0 copy-done.1
  64.0 0.0 copy-done.2
  64.0 0.0 copy-done.4
  64.0 0.0 copy-done.7
  64.0 91.7 %attend.1 = bf16[2048,256]{1,0:T(8,128)(2,1)} custom-call(s32[1,128]{1,0:T(1,128)S(1)} %get-tuple-element.16.summary_ref, s32[1]{0:T(128)} %bitcast.11.count_ref, bf16[2048,256]{1,0:T(8,128)(2,1)S(1)} %get-tuple-element.17.moved_ref, bf16[2048,256]{1,0:T(8,128)(2,1)S(1)} %get-tuple-element.18.normed_ref, bf16[1024,256]{1,0:T(8,128)(2,1)S(1)} %get-tuple-element.19.tail_ref, ...), custom_call_target="tpu_custom_call" | custom-call | tf_op jit(solution)/shard_map/attend/pallas_call | solution.py:512
Async XLA Ops:
  0.0 20.9 %copy-start.6 = (f32[256]{0:T(256)S(1)}, f32[256]{0:T(256)}, u32[]{:S(2)}) copy-start(f32[256]{0:T(256)} %param.20) | copy-start | bytes 3076
  0.0 20.9 %copy-start.5 = (f32[256]{0:T(256)S(1)}, f32[256]{0:T(256)}, u32[]{:S(2)}) copy-start(f32[256]{0:T(256)} %param.19) | copy-start | bytes 3076
  0.0 20.9 %copy-start.3 = (bf16[256,256]{1,0:T(8,128)(2,1)S(1)}, bf16[256,256]{1,0:T(8,128)(2,1)}, u32[]{:S(2)}) copy-start(bf16[256,256]{1,0:T(8,128)(2,1)} %cpe_ref.1) | copy-start | bytes 393220
  0.7 63.2 %copy-start = (bf16[256,1024]{1,0:T(8,128)(2,1)S(1)}, bf16[256,1024]{1,0:T(8,128)(2,1)}, u32[]{:S(2)}) copy-start(bf16[256,1024]{1,0:T(8,128)(2,1)} %fc_one_ref.1) | copy-start | bytes 1572868
  0.7 63.2 %copy-start.1 = (bf16[1024,256]{1,0:T(8,128)(2,1)S(1)}, bf16[1024,256]{1,0:T(8,128)(2,1)}, u32[]{:S(2)}) copy-start(bf16[1024,256]{1,0:T(8,128)(2,1)} %fc_two_ref.1) | copy-start | bytes 1572868
  0.7 63.2 %copy-start.2 = (bf16[256,768]{1,0:T(8,128)(2,1)S(1)}, bf16[256,768]{1,0:T(8,128)(2,1)}, u32[]{:S(2)}) copy-start(bf16[256,768]{1,0:T(8,128)(2,1)} %qkv_ref.1) | copy-start | bytes 1179652
  0.7 63.2 %copy-start.4 = (bf16[256,256]{1,0:T(8,128)(2,1)S(1)}, bf16[256,256]{1,0:T(8,128)(2,1)}, u32[]{:S(2)}) copy-start(bf16[256,256]{1,0:T(8,128)(2,1)} %proj_ref.1) | copy-start | bytes 393220
  0.7 63.2 %copy-start.7 = (f32[256]{0:T(256)S(1)}, f32[256]{0:T(256)}, u32[]{:S(2)}) copy-start(f32[256]{0:T(256)} %param.23) | copy-start | bytes 3076

commit v5 on v4

--- a/solution.py
+++ b/solution.py
@@ -274,28 +274,30 @@
         block = arrived_ref[order_ref[0, slot]]
         row = pl.multiple_of(slot * BLOCK, BLOCK)
         moved_ref[pl.ds(row, BLOCK), :] = block
+        put(wide_ref, row, block.astype(jnp.float32))
         return 0
 
-    lax.fori_loop(0, devices, settle, 0)
+    lax.fori_loop(0, devices, settle, 0, unroll=8)
     following = (me + 1) % devices
     previous = (me + devices - 1) % devices
     head_sems = (side_send_sem.at[0], side_recv_sem.at[0])
     tail_sems = (side_send_sem.at[1], side_recv_sem.at[1])
+    rows = devices * BLOCK
     head = to_peer(normed_ref.at[pl.ds(0, PATCH)], after_ref, head_sems, previous)
-    for part in range(moved_ref.shape[0] // QTILE):
-        here = slice(part * QTILE, (part + 1) * QTILE)
-        normed = normalised(moved_ref[here, :].astype(jnp.float32), gain_ref[...])
-        normed = normed.astype(jnp.bfloat16)
-        normed_ref[here, :] = normed
-        put(wide_ref, part * QTILE, normed.astype(jnp.float32))
-        if (part + 1) * QTILE == PATCH:
-            head.start()
-    start = jnp.clip(count_ref[0] - PATCH, 0, moved_ref.shape[0] - PATCH)
+    tail = to_peer(tail_ref, before_ref, tail_sems, following)
+    start = jnp.clip(count_ref[0] - PATCH, 0, rows - PATCH)
+
+    def first_norm(first):
+        return normalised(get(wide_ref, first, QTILE), gain_ref[...]).astype(jnp.bfloat16)
+
     for part in range(PATCH // QTILE):
-        piece = get(wide_ref, start + part * QTILE, QTILE)
-        tail_ref[part * QTILE : (part + 1) * QTILE, :] = piece.astype(jnp.bfloat16)
-    tail = to_peer(tail_ref, before_ref, tail_sems, following)
-    tail.start()
+        here = pl.ds(part * QTILE, QTILE)
+        tail_ref[here, :] = first_norm(start + part * QTILE)
+        to_peer(tail_ref.at[here], before_ref.at[here], tail_sems, following).start()
+        normed_ref[here, :] = first_norm(part * QTILE)
+        to_peer(normed_ref.at[here], after_ref.at[here], head_sems, previous).start()
+    for part in range(PATCH // QTILE, rows // QTILE):
+        normed_ref[pl.ds(part * QTILE, QTILE), :] = first_norm(part * QTILE)
     all_notes.wait_send()
     all_blocks.wait_send()
     head.wait()
@@ -452,14 +454,16 @@
         reach = jnp.max(squares(queries) * reach_ref[patch])
         safe = (reach <= SAFE_SCORE**2) & (jnp.max(size_ref[patch]) <= SAFE_VALUE)
 
-        def gather(group, odd, softened, so_far):
+        def grow(group, odd, softened):
             heads = [2 * (group * STACK + index) + odd for index in range(STACK)]
             one = jnp.concatenate(
                 [jnp.where(head_of_lane == head, queries, jnp.bfloat16(0)) for head in heads],
                 axis=0,
             )
             scores = jnp.dot(one, keys_ref[patch], preferred_element_type=jnp.float32)
-            grown = softened(scores).astype(jnp.bfloat16)
+            return heads, softened(scores).astype(jnp.bfloat16)
+
+        def gather(heads, odd, grown, so_far):
             mixed = jnp.dot(grown, values_ref[patch, odd], preferred_element_type=jnp.float32)
             spare = LANES - 1 if odd == 0 else 0
             mixed = mixed * (1.0 / mixed[:, spare : spare + 1])
@@ -470,11 +474,14 @@
 
         @pl.when(safe)
         def _():
+            steps = [(group, odd) for group in range(HEADS // (2 * STACK)) for odd in range(2)]
+            so_far = jnp.zeros((QTILE, width), jnp.float32)
+            ready = [grow(*steps[0], jnp.exp)]
             finish(before)
-            so_far = jnp.zeros((QTILE, width), jnp.float32)
-            for group in range(HEADS // (2 * STACK)):
-                for odd in range(2):
-                    so_far = gather(group, odd, jnp.exp, so_far)
+            for index, (_, odd) in enumerate(steps):
+                if index + 1 < len(steps):
+                    ready.append(grow(*steps[index + 1], jnp.exp))
+                so_far = gather(ready[index][0], odd, ready[index][1], so_far)
             gathered_ref[...] = so_far
 
         @pl.when(jnp.logical_not(safe))
@@ -490,7 +497,8 @@
             @pl.loop(0, HEADS // (2 * STACK))
             def _(group):
                 for odd in range(2):
-                    gathered_ref[...] = gather(group, odd, softened, gathered_ref[...])
+                    heads, grown = grow(group, odd, softened)
+                    gathered_ref[...] = gather(heads, odd, grown, gathered_ref[...])
 
     @pl.loop(live_tiles - 1, all_tiles)
     def _(tile):

time: 156 us -> 156 us (level)
  the two profiles are of different devices: /device:TPU:27 before, /device:TPU:24 now
where the time goes in v5:
time: 156 us
  Pallas kernels  155 us (99%)
    pallas_call x1, Pallas kernels, finished(): pl.pallas_call(block_kernel, out_shape=jax.ShapeDtypeStruct((rows, width)...  91.7 us
    pallas_call x1, Pallas kernels, exchanged(): pl.pallas_call(exchange_kernel, out_shape=(whole, whole, side, side, jax....  43.1 us
    pallas_call x1, Pallas kernels, convolved(): pl.pallas_call(conv_kernel, out_shape=(shape, shape, jax.ShapeDtypeStruct...  20.1 us

profile of v5, /device:TPU:24, one launch (start us, length us, event | category | flops | bytes accessed | tf_op | source)
XLA Modules:
  0.0 155.8 jit_solution(8294039794411913664)
XLA Ops:
  0.0 0.0 copy-start.6
  0.0 0.0 copy-start.5
  0.0 0.0 copy-start.3
  0.7 0.0 copy-start
  0.7 0.0 copy-start.1
  0.7 0.0 copy-start.2
  0.7 0.0 copy-start.4
  0.7 0.0 copy-start.7
  0.7 20.1 %convolve.1 = (bf16[128,16,256]{2,1,0:T(8,128)(2,1)S(1)}, bf16[128,16,256]{2,1,0:T(8,128)(2,1)S(1)}, s32[128,1,128]{2,1,0:T(1,128)S(1)}) custom-call(s32[128]{0:T(128)} %bitcast.18, s32[1]{0:T(128)} %bitcast.9.count_ref, s32[27,16,128]{2,1,0:T(8,128)} %bitcast.17, bf16[2048,256]{1,0:T(8,128)(2,1)} %bitcast.16, bf16[6912,256]{1,0:T(8,128)(2,1)} %bitcast.15), custom_call_target="tpu_custom_call" | custom-call | tf_op jit(solution)/shard_map/convolve/pallas_call | solution.py:138
  20.9 0.0 copy-done.6
  20.9 0.0 copy-done.5
  20.9 0.0 copy-done.3
  20.9 43.1 %exchange.1 = (bf16[2048,256]{1,0:T(8,128)(2,1)S(1)}, bf16[2048,256]{1,0:T(8,128)(2,1)S(1)}, bf16[1024,256]{1,0:T(8,128)(2,1)S(1)}, bf16[1024,256]{1,0:T(8,128)(2,1)S(1)}, s32[1,128]{1,0:T(1,128)S(1)}) custom-call(s32[1]{0:T(128)} %bitcast.10.count_ref, bf16[128,16,256]{2,1,0:T(8,128)(2,1)S(1)} %get-tuple-element.13.summed_ref, ...), custom_call_target="tpu_custom_call" | custom-call | tf_op jit(solution)/shard_map/exchange/pallas_call | solution.py:315
  64.1 0.0 copy-done
  64.1 0.0 copy-done.1
  64.1 0.0 copy-done.2
  64.1 0.0 copy-done.4
  64.1 0.0 copy-done.7
  64.1 91.7 %attend.1 = bf16[2048,256]{1,0:T(8,128)(2,1)} custom-call(s32[1,128]{1,0:T(1,128)S(1)} %get-tuple-element.16.summary_ref, s32[1]{0:T(128)} %bitcast.11.count_ref, bf16[2048,256]{1,0:T(8,128)(2,1)S(1)} %get-tuple-element.17.moved_ref, bf16[2048,256]{1,0:T(8,128)(2,1)S(1)} %get-tuple-element.18.normed_ref, bf16[1024,256]{1,0:T(8,128)(2,1)S(1)} %get-tuple-element.19.tail_ref, ...), custom_call_target="tpu_custom_call" | custom-call | tf_op jit(solution)/shard_map/attend/pallas_call | solution.py:520
Async XLA Ops:
  0.0 20.9 %copy-start.6 = (f32[256]{0:T(256)S(1)}, f32[256]{0:T(256)}, u32[]{:S(2)}) copy-start(f32[256]{0:T(256)} %param.20) | copy-start | bytes 3076
  0.0 20.9 %copy-start.5 = (f32[256]{0:T(256)S(1)}, f32[256]{0:T(256)}, u32[]{:S(2)}) copy-start(f32[256]{0:T(256)} %param.19) | copy-start | bytes 3076
  0.0 20.9 %copy-start.3 = (bf16[256,256]{1,0:T(8,128)(2,1)S(1)}, bf16[256,256]{1,0:T(8,128)(2,1)}, u32[]{:S(2)}) copy-start(bf16[256,256]{1,0:T(8,128)(2,1)} %cpe_ref.1) | copy-start | bytes 393220
  0.7 63.4 %copy-start = (bf16[256,1024]{1,0:T(8,128)(2,1)S(1)}, bf16[256,1024]{1,0:T(8,128)(2,1)}, u32[]{:S(2)}) copy-start(bf16[256,1024]{1,0:T(8,128)(2,1)} %fc_one_ref.1) | copy-start | bytes 1572868
  0.7 63.4 %copy-start.1 = (bf16[1024,256]{1,0:T(8,128)(2,1)S(1)}, bf16[1024,256]{1,0:T(8,128)(2,1)}, u32[]{:S(2)}) copy-start(bf16[1024,256]{1,0:T(8,128)(2,1)} %fc_two_ref.1) | copy-start | bytes 1572868
  0.7 63.4 %copy-start.2 = (bf16[256,768]{1,0:T(8,128)(2,1)S(1)}, bf16[256,768]{1,0:T(8,128)(2,1)}, u32[]{:S(2)}) copy-start(bf16[256,768]{1,0:T(8,128)(2,1)} %qkv_ref.1) | copy-start | bytes 1179652
  0.7 63.4 %copy-start.4 = (bf16[256,256]{1,0:T(8,128)(2,1)S(1)}, bf16[256,256]{1,0:T(8,128)(2,1)}, u32[]{:S(2)}) copy-start(bf16[256,256]{1,0:T(8,128)(2,1)} %proj_ref.1) | copy-start | bytes 393220
  0.7 63.4 %copy-start.7 = (f32[256]{0:T(256)S(1)}, f32[256]{0:T(256)}, u32[]{:S(2)}) copy-start(f32[256]{0:T(256)} %param.23) | copy-start | bytes 3076

commit v6 on v5

--- a/solution.py
+++ b/solution.py
@@ -238,7 +238,7 @@
         outgoing_ref[here] = encoded.reshape(QTILE // BLOCK, BLOCK, -1)
         return 0
 
-    lax.fori_loop(0, devices * BLOCK // QTILE, encode, 0)
+    lax.fori_loop(0, devices * BLOCK // QTILE, encode, 0, unroll=4)
     pl.semaphore_wait(barrier, devices - 1)
 
     def send(step, _):

time: 156 us -> 155 us (level)
  the two profiles are of different devices: /device:TPU:24 before, /device:TPU:26 now
where the time goes in v6:
time: 155 us; the launch traced here: 154 us
  Pallas kernels  154 us (99%)
    pallas_call x1, Pallas kernels, finished(): pl.pallas_call(block_kernel, out_shape=jax.ShapeDtypeStruct((rows, width)...  91.7 us
    pallas_call x1, Pallas kernels, exchanged(): pl.pallas_call(exchange_kernel, out_shape=(whole, whole, side, side, jax....  41.7 us
    pallas_call x1, Pallas kernels, convolved(): pl.pallas_call(conv_kernel, out_shape=(shape, shape, jax.ShapeDtypeStruct...  20.1 us

profile of v6, /device:TPU:26, one launch (start us, length us, event | category | flops | bytes accessed | tf_op | source)
XLA Modules:
  0.0 154.4 jit_solution(3975261726728552646)
XLA Ops:
  0.0 0.0 copy-start.6
  0.0 0.0 copy-start.5
  0.0 0.0 copy-start.3
  0.7 0.0 copy-start
  0.7 0.0 copy-start.1
  0.7 0.0 copy-start.2
  0.7 0.0 copy-start.4
  0.7 0.0 copy-start.7
  0.7 20.1 %convolve.1 = (bf16[128,16,256]{2,1,0:T(8,128)(2,1)S(1)}, bf16[128,16,256]{2,1,0:T(8,128)(2,1)S(1)}, s32[128,1,128]{2,1,0:T(1,128)S(1)}) custom-call(s32[128]{0:T(128)} %bitcast.18, s32[1]{0:T(128)} %bitcast.9.count_ref, s32[27,16,128]{2,1,0:T(8,128)} %bitcast.17, bf16[2048,256]{1,0:T(8,128)(2,1)} %bitcast.16, bf16[6912,256]{1,0:T(8,128)(2,1)} %bitcast.15), custom_call_target="tpu_custom_call" | custom-call | tf_op jit(solution)/shard_map/convolve/pallas_call | solution.py:138
  20.9 0.0 copy-done.6
  20.9 0.0 copy-done.5
  20.9 0.0 copy-done.3
  20.9 41.7 %exchange.1 = (bf16[2048,256]{1,0:T(8,128)(2,1)S(1)}, bf16[2048,256]{1,0:T(8,128)(2,1)S(1)}, bf16[1024,256]{1,0:T(8,128)(2,1)S(1)}, bf16[1024,256]{1,0:T(8,128)(2,1)S(1)}, s32[1,128]{1,0:T(1,128)S(1)}) custom-call(s32[1]{0:T(128)} %bitcast.10.count_ref, bf16[128,16,256]{2,1,0:T(8,128)(2,1)S(1)} %get-tuple-element.13.summed_ref, ...), custom_call_target="tpu_custom_call" | custom-call | tf_op jit(solution)/shard_map/exchange/pallas_call | solution.py:315
  62.6 0.0 copy-done
  62.6 0.0 copy-done.1
  62.7 0.0 copy-done.2
  62.7 0.0 copy-done.4
  62.7 0.0 copy-done.7
  62.7 91.7 %attend.1 = bf16[2048,256]{1,0:T(8,128)(2,1)} custom-call(s32[1,128]{1,0:T(1,128)S(1)} %get-tuple-element.16.summary_ref, s32[1]{0:T(128)} %bitcast.11.count_ref, bf16[2048,256]{1,0:T(8,128)(2,1)S(1)} %get-tuple-element.17.moved_ref, bf16[2048,256]{1,0:T(8,128)(2,1)S(1)} %get-tuple-element.18.normed_ref, bf16[1024,256]{1,0:T(8,128)(2,1)S(1)} %get-tuple-element.19.tail_ref, ...), custom_call_target="tpu_custom_call" | custom-call | tf_op jit(solution)/shard_map/attend/pallas_call | solution.py:520
Async XLA Ops:
  0.0 20.9 %copy-start.6 = (f32[256]{0:T(256)S(1)}, f32[256]{0:T(256)}, u32[]{:S(2)}) copy-start(f32[256]{0:T(256)} %param.20) | copy-start | bytes 3076
  0.0 20.9 %copy-start.5 = (f32[256]{0:T(256)S(1)}, f32[256]{0:T(256)}, u32[]{:S(2)}) copy-start(f32[256]{0:T(256)} %param.19) | copy-start | bytes 3076
  0.0 20.9 %copy-start.3 = (bf16[256,256]{1,0:T(8,128)(2,1)S(1)}, bf16[256,256]{1,0:T(8,128)(2,1)}, u32[]{:S(2)}) copy-start(bf16[256,256]{1,0:T(8,128)(2,1)} %cpe_ref.1) | copy-start | bytes 393220
  0.7 61.9 %copy-start = (bf16[256,1024]{1,0:T(8,128)(2,1)S(1)}, bf16[256,1024]{1,0:T(8,128)(2,1)}, u32[]{:S(2)}) copy-start(bf16[256,1024]{1,0:T(8,128)(2,1)} %fc_one_ref.1) | copy-start | bytes 1572868
  0.7 61.9 %copy-start.1 = (bf16[1024,256]{1,0:T(8,128)(2,1)S(1)}, bf16[1024,256]{1,0:T(8,128)(2,1)}, u32[]{:S(2)}) copy-start(bf16[1024,256]{1,0:T(8,128)(2,1)} %fc_two_ref.1) | copy-start | bytes 1572868
  0.7 61.9 %copy-start.2 = (bf16[256,768]{1,0:T(8,128)(2,1)S(1)}, bf16[256,768]{1,0:T(8,128)(2,1)}, u32[]{:S(2)}) copy-start(bf16[256,768]{1,0:T(8,128)(2,1)} %qkv_ref.1) | copy-start | bytes 1179652
  0.7 61.9 %copy-start.4 = (bf16[256,256]{1,0:T(8,128)(2,1)S(1)}, bf16[256,256]{1,0:T(8,128)(2,1)}, u32[]{:S(2)}) copy-start(bf16[256,256]{1,0:T(8,128)(2,1)} %proj_ref.1) | copy-start | bytes 393220
  0.7 61.9 %copy-start.7 = (f32[256]{0:T(256)S(1)}, f32[256]{0:T(256)}, u32[]{:S(2)}) copy-start(f32[256]{0:T(256)} %param.23) | copy-start | bytes 3076
